TPU v7x, 128 devices: a whole 4x4x4 slice. The times are simulated.
128 devices in a mesh: gen: 32 (over y, z, core), grp: 4 (over x).
Axes of the slice: x: 4, y: 4, z: 4, core: 2. Of those that a mesh axis runs over, the one named last changes fastest.
Arguments:
- query_in: bfloat16 [4, 4096, 4096], P('grp', 'gen'), may hold values from -8 to 8, as said below
- key_in: bfloat16 [4, 4096, 4096], P('grp', 'gen'), may hold values from -8 to 8
- value_in: bfloat16 [4, 4096, 4096], P('grp', 'gen'), may hold values from -6 to 6
- teacher_w: bfloat16 [4096, 5120], P('gen'), may hold values from -0.09375 to 0.09375
- disc_heads: float32 [8, 5120], replicated, may hold values from -0.078125 to 0.078125
- frame_of_token: int32 [4, 4096], P('grp'), may hold values from 0 to 20, never falling along the last dimension, each value on 1 to 390 neighbouring positions
- head_of_frame: int32 [4, 21], P('grp'), may hold values from 0 to 7
- timestep: int32 [4], P('grp'), may hold values from 0 to 999
Outputs:
- latents: bfloat16 [4, 4096, 4096], P('grp', 'gen')
- grad_query: bfloat16 [4, 4096, 4096], P('grp', 'gen')
- grad_key: bfloat16 [4, 4096, 4096], P('grp', 'gen')
- grad_value: bfloat16 [4, 4096, 4096], P('grp', 'gen')
- grad_heads: float32 [8, 5120], replicated
Inputs may be any that keep to these rules, and one draw needn't show every extreme that they name: `query_in`: entries lie within the range; in some draws a few queries equal some keys. `frame_of_token`: within a clip the frame numbers never fall along the tokens; every frame holds 1 to 390 tokens and some frame exactly 390.
All inputs are finite; a program needn't handle non-finite values.
Results may differ from a plain program's by a relative error of at most 0.035.
Values may be sent and summed in bfloat16 or wider, within the bound.
A program may use at most 64 MiB of HBM per device.

v0:
```python
import math

import jax
import jax.numpy as jnp
from jax import lax
from jax.sharding import PartitionSpec as P

HS = 128
FRAMES = 21
NDH = 8
NSTEPS = 1000


epsilon = 1e-06


def forward_rows(query_rows, key_three, value_three):
    inv_scale = 1.0 / math.sqrt(HS)
    scores = (
        jnp.einsum("rhd,thd->hrt", query_rows, key_three, preferred_element_type=jnp.float32)
        * inv_scale
    )
    peak = jnp.max(scores, axis=2, keepdims=True)
    weights = jnp.exp(scores - peak)
    total = jnp.sum(weights, axis=2, keepdims=True)
    mixed = jnp.einsum(
        "hrt,thd->rhd",
        weights.astype(jnp.bfloat16),
        value_three,
        preferred_element_type=jnp.float32,
    )
    mixed = mixed / jnp.transpose(total, (1, 0, 2))
    lse_rows = jnp.transpose((peak + jnp.log(total))[:, :, 0], (1, 0))
    return (mixed.astype(jnp.bfloat16), lse_rows)


def backward_rows(carry, items, key_three, value_three):
    inv_scale = 1.0 / math.sqrt(HS)
    grad_key, grad_value = carry
    query_rows, lse_rows, grad_rows, delta_rows = items
    scores = (
        jnp.einsum("rhd,thd->hrt", query_rows, key_three, preferred_element_type=jnp.float32)
        * inv_scale
    )
    probs = jnp.exp(scores - jnp.transpose(lse_rows, (1, 0))[:, :, None])
    grad_value = grad_value + jnp.einsum(
        "hrt,rhd->thd", probs.astype(jnp.bfloat16), grad_rows, preferred_element_type=jnp.float32
    )
    grad_probs = jnp.einsum(
        "rhd,thd->hrt", grad_rows, value_three, preferred_element_type=jnp.float32
    )
    dscore = (
        probs * (grad_probs - jnp.transpose(delta_rows, (1, 0))[:, :, None]) * inv_scale
    ).astype(jnp.bfloat16)
    grad_query = jnp.einsum(
        "hrt,thd->rhd", dscore, key_three, preferred_element_type=jnp.float32
    ).astype(jnp.bfloat16)
    grad_key = grad_key + jnp.einsum(
        "hrt,rhd->thd", dscore, query_rows, preferred_element_type=jnp.float32
    )
    return ((grad_key, grad_value), grad_query)


def on_device(
    query_in, key_in, value_in, teacher_w, disc_heads, frame_of_token, head_of_frame, timestep
):
    group = lax.axis_size("gen")
    tok_dev = query_in.shape[1]
    width = query_in.shape[2]
    tokens = tok_dev * group
    heads_dev = width // HS // group
    local_width = heads_dev * HS
    row_block = min(512, tokens)
    block_count = tokens // row_block
    seq_rows = (query_in[0], key_in[0], value_in[0])
    head_query, head_key, head_value = (
        lax.all_to_all(seq_rows[0], "gen", split_axis=1, concat_axis=0, tiled=True),
        lax.all_to_all(seq_rows[1], "gen", split_axis=1, concat_axis=0, tiled=True),
        lax.all_to_all(seq_rows[2], "gen", split_axis=1, concat_axis=0, tiled=True),
    )
    key_three = head_key.reshape(tokens, heads_dev, HS)
    value_three = head_value.reshape(tokens, heads_dev, HS)

    def forward_block(query_rows):
        return forward_rows(query_rows, key_three, value_three)

    mixed_blocks, lse_blocks = lax.map(
        forward_block, head_query.reshape(block_count, row_block, heads_dev, HS)
    )
    mixed = mixed_blocks.reshape(tokens, local_width)
    latents = lax.all_to_all(mixed, "gen", split_axis=0, concat_axis=1, tiled=True)
    frames = frame_of_token[0]
    frame_ids = lax.broadcasted_iota(jnp.int32, (FRAMES, tokens), 0)
    member = frames[None, :] == frame_ids
    counts = jnp.sum(member.astype(jnp.float32), axis=1)
    pooled = (
        jnp.dot(member.astype(jnp.bfloat16), mixed, preferred_element_type=jnp.float32)
        / counts[:, None]
    )
    square_part = jnp.sum(pooled * pooled, axis=1)
    project_part = jnp.dot(
        pooled.astype(jnp.bfloat16), teacher_w, preferred_element_type=jnp.float32
    )
    head_ids = lax.broadcasted_iota(jnp.int32, (FRAMES, NDH), 1)
    picked = (head_of_frame[0][:, None] == head_ids).astype(jnp.float32)
    head_rows = jnp.dot(picked, disc_heads, precision=lax.Precision.HIGHEST)
    weight = (timestep[0].astype(jnp.float32) + 1.0) / NSTEPS
    projected, squares = (
        lax.psum(project_part.astype(jnp.bfloat16), "gen").astype(jnp.float32),
        lax.psum(square_part.astype(jnp.bfloat16), "gen").astype(jnp.float32),
    )
    root = jnp.sqrt(squares / width + epsilon)
    pre = projected / root[:, None]
    gate = jax.nn.sigmoid(pre)
    feature = pre * gate
    score = jnp.sum(feature * head_rows, axis=1)
    grad_score = -weight * jax.nn.sigmoid(-score) / FRAMES
    head_part = jnp.dot(picked.T, grad_score[:, None] * feature, precision=lax.Precision.HIGHEST)
    grad_pre = grad_score[:, None] * head_rows * gate * (1.0 + pre * (1.0 - gate))
    grad_projected = (grad_pre / root[:, None]).astype(jnp.bfloat16)
    grad_root = -jnp.sum(grad_pre * pre, axis=1) / root
    grad_heads = lax.psum(head_part.astype(jnp.bfloat16), "grp").astype(jnp.float32)
    grad_pooled = (
        jnp.dot(grad_projected, teacher_w.T, preferred_element_type=jnp.float32)
        + (grad_root / root / width)[:, None] * pooled
    )
    spread = grad_pooled / counts[:, None]
    grad_mixed = (tokens * jnp.take(spread, frames, axis=0)).astype(jnp.bfloat16)
    product = grad_mixed.astype(jnp.float32) * mixed.astype(jnp.float32)
    delta = jnp.sum(product.reshape(tokens, heads_dev, HS), axis=2)
    back_query, back_key, back_value = (head_query, head_key, head_value)
    back_key_three = back_key.reshape(tokens, heads_dev, HS)
    back_value_three = back_value.reshape(tokens, heads_dev, HS)

    def back_block(carry, items):
        return backward_rows(carry, items, back_key_three, back_value_three)

    block_items = (
        back_query.reshape(block_count, row_block, heads_dev, HS),
        lse_blocks,
        grad_mixed.reshape(block_count, row_block, heads_dev, HS),
        delta.reshape(block_count, row_block, heads_dev),
    )
    zeros_start = jnp.zeros((tokens, heads_dev, HS), jnp.float32)
    sums_out, query_blocks = lax.scan(back_block, (zeros_start, zeros_start), block_items)
    grads = (
        query_blocks.reshape(tokens, local_width),
        sums_out[0].astype(jnp.bfloat16).reshape(tokens, local_width),
        sums_out[1].astype(jnp.bfloat16).reshape(tokens, local_width),
    )
    out_query, out_key, out_value = (
        lax.all_to_all(grads[0], "gen", split_axis=0, concat_axis=1, tiled=True),
        lax.all_to_all(grads[1], "gen", split_axis=0, concat_axis=1, tiled=True),
        lax.all_to_all(grads[2], "gen", split_axis=0, concat_axis=1, tiled=True),
    )
    return (latents[None], out_query[None], out_key[None], out_value[None], grad_heads)


def solution(mesh):
    return jax.shard_map(
        on_device,
        mesh=mesh,
        in_specs=(
            P("grp", "gen", None),
            P("grp", "gen", None),
            P("grp", "gen", None),
            P("gen", None),
            P(),
            P("grp", None),
            P("grp", None),
            P("grp"),
        ),
        out_specs=(
            P("grp", "gen", None),
            P("grp", "gen", None),
            P("grp", "gen", None),
            P("grp", "gen", None),
            P(),
        ),
        check_vma=False,
    )
```

profile of v0, /device:TPU:1, one launch (start us, length us, event | category | flops | bytes accessed | tf_op | source)
XLA Modules:
  0.0 551.7 jit_solution(15540477123714850966)
XLA Ops:
  9.6 9.6 %all-to-all-start = ((bf16[128,32,128]{0,2,1:T(8,128)(2,1)}), bf16[128,32,128]{0,2,1:T(8,128)(2,1)S(1)}, u32[]{:S(2)}, u32[]{:S(2)}) async-start(bf16[128,32,128]{0,2,1:T(8,128)(2,1)} %bitcast.8), calls=%async_computation | async-start | bytes 2097152 | tf_op jit(solution)/shard_map/all_to_all | solution.py:77
  20.5 15.6 %all-to-all-done = bf16[128,32,128]{0,2,1:T(8,128)(2,1)S(1)} async-done(((bf16[128,32,128]{0,2,1:T(8,128)(2,1)}), bf16[128,32,128]{0,2,1:T(8,128)(2,1)S(1)}, u32[]{:S(2)}, u32[]{:S(2)}) %all-to-all-start) | async-done | bytes 1048608 | tf_op jit(solution)/shard_map/all_to_all | solution.py:77
  36.1 4.0 all-to-all-start.1
  44.5 12.6 %all-to-all-done.1 = bf16[128,32,128]{0,2,1:T(8,128)(2,1)S(1)} async-done(((bf16[128,32,128]{0,2,1:T(8,128)(2,1)}), bf16[128,32,128]{0,2,1:T(8,128)(2,1)S(1)}, u32[]{:S(2)}, u32[]{:S(2)}) %all-to-all-start.1) | async-done | bytes 1048608 | tf_op jit(solution)/shard_map/all_to_all | solution.py:78
  57.0 4.4 all-to-all-start.2
  63.5 15.0 %all-to-all-done.2 = bf16[128,32,128]{0,2,1:T(8,128)(2,1)} async-done(((bf16[128,32,128]{0,2,1:T(8,128)(2,1)}), bf16[128,32,128]{0,2,1:T(8,128)(2,1)}, u32[]{:S(2)}, u32[]{:S(2)}) %all-to-all-start.2) | async-done | bytes 1048608 | tf_op jit(solution)/shard_map/all_to_all | solution.py:79
  81.2 47.3 %while.27 = (s32[]{:T(128)}, bf16[8,512,1,128]{3,1,2,0:T(8,128)(2,1)}, f32[8,512,1]{1,2,0:T(1,128)S(1)}, bf16[8,512,1,128]{3,1,2,0:T(8,128)(2,1)}, bf16[4096,1,1...) while((s32[]{:T(128)}, bf16[8,512,1,128]{3,1,2,0:T(8,128)(2,1)}, ...), condition=%wide.region_3.4_spmd, body=%wide.region_0.3_spmd.sunk | while | flops 1090649600 | bytes 27545696 | solution.py:87
  128.5 4.6 all-to-all-start.3
  134.7 69.7 %psum.22 = bf16[21]{0:T(256)(128)(2,1)S(1)} all-reduce(bf16[21]{0:T(256)(128)(2,1)S(1)} %get-tuple-element.256), channel_id=1, replica_groups=mesh['gen'=32,'grp'=4] {'gen'}, use_global_device_ids=true, to_apply=%region_7.8 | all-reduce | flops 21 | bytes 84 | tf_op jit(solution)/shard_map/psum | solution.py:110
  205.4 97.3 %all-reduce.3.cloned.1.call-done = bf16[21,5120]{1,0:T(8,128)(2,1)} async-done(((bf16[21,5120]{1,0:T(8,128)(2,1)}), bf16[21,5120]{1,0:T(8,128)(2,1)}) %all-reduce.3.cloned.1.call-update) | async-done | bytes 215056 | tf_op jit(solution)/shard_map/psum | solution.py:109
  305.4 14.1 %gather_fusion = f32[4096,128]{1,0:T(8,128)} fusion(f32[21,128]{1,0:T(8,128)S(1)} %fusion.54, s32[4096]{0:T(1024)S(1)} %broadcast_clamp_fusion), kind=kCustom, calls=%fused_computation | custom fusion | bytes 4210688 | tf_op jit(solution)/shard_map/jit(_take)/gather | solution.py:128
  325.4 113.5 %while.28 = (s32[]{:T(128)}, f32[4096,1,128]{0,2,1:T(8,128)}, f32[4096,1,128]{0,2,1:T(8,128)}, bf16[8,512,1,128]{3,1,2,0:T(8,128)(2,1)}, bf16[8,512,1,128]{3,1,2...) while((s32[]{:T(128)}, f32[4096,1,128]{0,2,1:T(8,128)}, ...), condition=%wide.region_12.13_spmd.clone, body=%wide.region_11.12_spmd.clone.sunk | while | flops 2705391616 | bytes 83507480 | solution.py:145
  327.7 2.9 fusion.107
  330.6 3.6 multiply_convert_fusion.3
  341.9 2.9 fusion.107
  344.8 3.6 multiply_convert_fusion.3
  356.1 2.9 fusion.107
  359.0 3.6 multiply_convert_fusion.3
  370.3 2.9 fusion.107
  373.2 3.6 multiply_convert_fusion.3
  384.5 2.9 fusion.107
  387.4 3.6 multiply_convert_fusion.3
  401.6 3.6 multiply_convert_fusion.3
  415.8 3.6 multiply_convert_fusion.3
  427.0 2.9 fusion.107
  430.0 3.6 multiply_convert_fusion.3
  438.9 6.1 %all-to-all-start.4 = ((bf16[32,128,128]{2,1,0:T(8,128)(2,1)}), bf16[32,128,128]{2,1,0:T(8,128)(2,1)S(1)}, u32[]{:S(2)}, u32[]{:S(2)}) async-start(bf16[32,128,128]{2,1,0:T(8,128)(2,1)} %bitcast.182), calls=%async_computation.4 | async-start | bytes 2097152 | tf_op jit(solution)/shard_map/all_to_all | solution.py:152
  448.0 13.9 %all-to-all-done.4 = bf16[32,128,128]{2,1,0:T(8,128)(2,1)S(1)} async-done(((bf16[32,128,128]{2,1,0:T(8,128)(2,1)}), bf16[32,128,128]{2,1,0:T(8,128)(2,1)S(1)}, u32[]{:S(2)}, u32[]{:S(2)}) %all-to-all-start.4) | async-done | bytes 1048608 | tf_op jit(solution)/shard_map/all_to_all | solution.py:152
  461.9 4.5 all-to-all-start.5
  469.4 13.9 %all-to-all-done.5 = bf16[32,128,128]{2,1,0:T(8,128)(2,1)} async-done(((bf16[32,128,128]{2,1,0:T(8,128)(2,1)}), bf16[32,128,128]{2,1,0:T(8,128)(2,1)}, u32[]{:S(2)}, u32[]{:S(2)}) %all-to-all-start.5) | async-done | bytes 1048608 | tf_op jit(solution)/shard_map/all_to_all | solution.py:153
  483.4 3.9 all-to-all-start.6
  489.7 40.6 %all-reduce.5.cloned.1.call-done = bf16[8,5120]{1,0:T(8,128)(2,1)} async-done(((bf16[8,5120]{1,0:T(8,128)(2,1)}), bf16[8,5120]{1,0:T(8,128)(2,1)}) %all-reduce.5.cloned.1.call-update) | async-done | bytes 81936 | tf_op jit(solution)/shard_map/psum | solution.py:122
  (199 shorter events, 160.1 us)
Async XLA Ops:
  7.2 197.2 %copy-start = (bf16[128,5120]{1,0:T(8,128)(2,1)S(1)}, bf16[128,5120]{1,0:T(8,128)(2,1)}, u32[]{:S(2)}) copy-start(bf16[128,5120]{1,0:T(8,128)(2,1)} %param.15) | copy-start | bytes 3932164
  7.2 12.0 %copy-start.6 = (bf16[1,128,4096]{2,1,0:T(8,128)(2,1)S(1)}, bf16[1,128,4096]{2,1,0:T(8,128)(2,1)}, u32[]{:S(2)}) copy-start(bf16[1,128,4096]{2,1,0:T(8,128)(2,1)} %param.13) | copy-start | bytes 3145732
  7.2 34.1 %copy-start.7 = (s32[1,4096]{1,0:T(1,128)S(1)}, s32[1,4096]{1,0:T(1,128)}, u32[]{:S(2)}) copy-start(s32[1,4096]{1,0:T(1,128)} %param.17) | copy-start | bytes 49156
  9.6 26.5 %all-to-all-start = ((bf16[128,32,128]{0,2,1:T(8,128)(2,1)}), bf16[128,32,128]{0,2,1:T(8,128)(2,1)S(1)}, u32[]{:S(2)}, u32[]{:S(2)}) async-start(bf16[128,32,128]{0,2,1:T(8,128)(2,1)} %bitcast.8), calls=%async_computation | async-start | bytes 2097152 | tf_op jit(solution)/shard_map/all_to_all | solution.py:77
  36.1 20.9 %all-to-all-start.1 = ((bf16[128,32,128]{0,2,1:T(8,128)(2,1)}), bf16[128,32,128]{0,2,1:T(8,128)(2,1)S(1)}, u32[]{:S(2)}, u32[]{:S(2)}) async-start(bf16[128,32,128]{0,2,1:T(8,128)(2,1)} %bitcast.179), calls=%async_computation.1 | async-start | bytes 2097152 | tf_op jit(solution)/shard_map/all_to_all | solution.py:78
  57.0 21.4 %all-to-all-start.2 = ((bf16[128,32,128]{0,2,1:T(8,128)(2,1)}), bf16[128,32,128]{0,2,1:T(8,128)(2,1)}, u32[]{:S(2)}, u32[]{:S(2)}) async-start(bf16[128,32,128]{0,2,1:T(8,128)(2,1)} %bitcast.180), calls=%async_computation.2 | async-start | bytes 2097152 | tf_op jit(solution)/shard_map/all_to_all | solution.py:79
  128.5 174.3 %copy-start.9 = (s32[1,21]{1,0:T(1,128)S(1)}, s32[1,21]{1,0:T(1,128)}, u32[]{:S(2)}) copy-start(s32[1,21]{1,0:T(1,128)} %param.18) | copy-start | bytes 256
  128.5 310.5 %all-to-all-start.3 = ((bf16[32,128,128]{2,1,0:T(8,128)(2,1)}), bf16[32,128,128]{2,1,0:T(8,128)(2,1)}, u32[]{:S(2)}, u32[]{:S(2)}) async-start(bf16[32,128,128]{2,1,0:T(8,128)(2,1)} %bitcast.172), calls=%async_computation.3 | async-start | bytes 2097152 | tf_op jit(solution)/shard_map/all_to_all | solution.py:91
  133.1 169.6 %all-reduce.3.cloned.1.call-start = ((), (), s32[]{:S(2)}) async-start(), calls=%async_computation.7 | async-start | bytes 491520 | tf_op jit(solution)/shard_map/psum | solution.py:109
  319.5 2.8 copy-start.5
  325.4 2.3 copy-start.3
  330.6 3.6 copy-start.4
  339.6 2.3 copy-start.3
  344.8 3.6 copy-start.4
  348.5 1.9 copy-start.1
  353.8 2.3 copy-start.3
  359.0 3.6 copy-start.4
  362.7 1.9 copy-start.1
  368.0 2.3 copy-start.3
  373.2 3.6 copy-start.4
  382.2 2.3 copy-start.3
  387.4 3.6 copy-start.4
  396.3 2.3 copy-start.3
  401.6 3.6 copy-start.4
  410.5 2.3 copy-start.3
  415.8 3.6 copy-start.4
  424.7 2.3 copy-start.3
  430.0 3.6 copy-start.4
  438.9 23.0 %all-to-all-start.4 = ((bf16[32,128,128]{2,1,0:T(8,128)(2,1)}), bf16[32,128,128]{2,1,0:T(8,128)(2,1)S(1)}, u32[]{:S(2)}, u32[]{:S(2)}) async-start(bf16[32,128,128]{2,1,0:T(8,128)(2,1)} %bitcast.182), calls=%async_computation.4 | async-start | bytes 2097152 | tf_op jit(solution)/shard_map/all_to_all | solution.py:152
  461.9 21.4 %all-to-all-start.5 = ((bf16[32,128,128]{2,1,0:T(8,128)(2,1)}), bf16[32,128,128]{2,1,0:T(8,128)(2,1)}, u32[]{:S(2)}, u32[]{:S(2)}) async-start(bf16[32,128,128]{2,1,0:T(8,128)(2,1)} %bitcast.181), calls=%async_computation.5 | async-start | bytes 2097152 | tf_op jit(solution)/shard_map/all_to_all | solution.py:153
  483.4 59.5 %all-to-all-start.6 = ((bf16[32,128,128]{2,1,0:T(8,128)(2,1)}), bf16[32,128,128]{2,1,0:T(8,128)(2,1)S(1)}, u32[]{:S(2)}, u32[]{:S(2)}) async-start(bf16[32,128,128]{2,1,0:T(8,128)(2,1)} %bitcast.178), calls=%async_computation.6 | async-start | bytes 2097152 | tf_op jit(solution)/shard_map/all_to_all | solution.py:154
  487.3 43.0 %all-reduce.5.cloned.1.call-start = ((), (), s32[]{:S(2)}) async-start(), calls=%async_computation.8 | async-start | bytes 163840 | tf_op jit(solution)/shard_map/psum | solution.py:122
  (15 other events, 24.0 us)
Sparse Core Ops, SparseCore 0:
  205.5 97.1 all-reduce.2
  491.1 39.0 all-reduce.4
where the time goes:
time: 555 us; the launch traced here: 552 us
  waiting for transfers between devices  209 us (38%)
  matrix products  144 us (26%)
  blocking collectives  69.7 us (13%)
  local copies, waits for them, and re-layouts  52.8 us (10%)
  starting transfers between devices  37.4 us (7%)
  other arithmetic  23.3 us (4%)
  between operations  14.9 us (3%)
    psum x1, waiting for transfers between devices, on_device(): lax.psum(project_part.astype(jnp.bfloat16), 'gen').astype(jnp.float32)  97.3 us
    psum x1, blocking collectives, on_device(): lax.psum(square_part.astype(jnp.bfloat16), 'gen').astype(jnp.float32)  69.7 us
    psum x1, waiting for transfers between devices, on_device(): lax.psum(head_part.astype(jnp.bfloat16), 'grp').astype(jnp.float32)  40.6 us
    dot_general x8, matrix products, backward_rows(): jnp.einsum('rhd,thd->hrt', grad_rows, value_three, preferred_element_type...  29 us
    dot_general x8, matrix products, backward_rows(): jnp.einsum('hrt,rhd->thd', probs.astype(jnp.bfloat16), grad_rows, preferr...  23.3 us
    dot_general x8, matrix products, backward_rows(): jnp.einsum('rhd,thd->hrt', query_rows, key_three, preferred_element_type=...  18.4 us
    dot_general x8, matrix products, forward_rows(): jnp.einsum('rhd,thd->hrt', query_rows, key_three, preferred_element_type=...  17.9 us
    dot_general x8, matrix products, forward_rows(): jnp.einsum('hrt,thd->rhd', weights.astype(jnp.bfloat16), value_three, pre...  17.2 us
  transfers between devices with their start and end apart: 9, of which 7 were waited for; matrix products, arithmetic and copies ran while one was open for 28% of the time, Pallas kernels for 0%

commit v1 on v0

v1 whole, which is shorter than its diff:
```python
import functools
import math

import jax
import jax.numpy as jnp
from jax import lax
from jax.experimental import pallas as pl
from jax.experimental.pallas import tpu as pltpu
from jax.sharding import PartitionSpec as P

HS = 128
FRAMES = 21
NDH = 8
NSTEPS = 1000
EPS = 1e-06
GEN = 32
GRP = 4
TOK = 4096
TD = 128
DH = 5120
FP = 32
OT = 256
OWN = 21
MESH = pl.DeviceIdType.MESH
f32 = jnp.float32
bf16 = jnp.bfloat16
NT = (((1,), (1,)), ((), ()))
NN = (((1,), (0,)), ((), ()))
TN = (((0,), (0,)), ((), ()))
CHIPS = [
    (2, 2), (3, 2), (2, 3), (1, 2), (2, 1), (0, 2), (2, 0), (3, 1), (1, 3), (3, 3), (1, 1),
    (0, 3), (0, 1), (3, 0), (1, 0),
]
FAR = [(dy, dz, dc) for dy, dz in CHIPS for dc in (0, 1)] + [(0, 0, 1)]


def mm(a, b, dims):
    return lax.dot_general(a, b, dims, preferred_element_type=f32)


def body(
    q_in, k_in, v_in, w_ref, disc_ref, frames_ref, hof_ref, time_ref,
    lat_out, dq_out, dk_out, dv_out, gh_out,
    probs, qh, kh, vh, oh, sa, sb, dkt, qwt, wrow, member, memberl, rbuf, r_all, g_src, g_all,
    rs_src, rs_recv, ag_src, proj, head_rows, gsf, hp_src, hp_all,
    sem_send, sem_q, sem_recv,
):
    g = lax.axis_index("gen")
    x = lax.axis_index("grp")
    y = g // 8
    z = (g // 2) % 4
    c = g % 2
    chip = g // 2

    def peer(off):
        dy, dz, dc = off
        ey = dy + c * (dz - dy)
        ez = dz + c * (dy - dz)
        return ((y + ey) % 4) * 8 + ((z + ez) % 4) * 2 + (c + dc) % 2

    def rows(i, n):
        return pl.ds(pl.multiple_of(i * n, n), n)

    def remote(src, dst, send, recv, dev):
        return pltpu.make_async_remote_copy(
            src_ref=src, dst_ref=dst, send_sem=send, recv_sem=recv,
            device_id={"gen": dev}, device_id_type=MESH,
        )

    def drain(ref, sem):
        pltpu.make_async_copy(ref, ref, sem).wait()

    barrier = pltpu.get_barrier_semaphore()
    for off in FAR:
        pl.semaphore_signal(barrier, inc=1, device_id={"gen": peer(off)}, device_id_type=MESH)
    for d in range(1, GRP):
        pl.semaphore_signal(
            barrier, inc=1, device_id={"grp": (x + d) % GRP}, device_id_type=MESH
        )
    pl.semaphore_wait(barrier, GEN - 1 + GRP - 1)

    for src, dst, which in ((k_in, kh, 0), (v_in, vh, 1)):
        pltpu.make_async_copy(src.at[:, rows(g, TD)], dst.at[rows(g, TD), :], sem_recv.at[which]).start()
        for off in FAR:
            p = peer(off)
            remote(
                src.at[:, rows(p, TD)], dst.at[rows(g, TD), :],
                sem_send.at[which], sem_recv.at[which], p,
            ).start()

    def q_chip(i, sign):
        dy = i % 4
        dz = (i // 4 + i) % 4
        return ((y + sign * dy + 4) % 4) * 4 + (z + sign * dz + 4) % 4

    pltpu.make_async_copy(q_in.at[:, rows(g, TD)], qh.at[rows(g, TD), :], sem_q.at[0]).start()
    for i in range(16):
        for dc in (0, 1):
            if i == 0 and dc == 0:
                continue
            p = q_chip(i, 1) * 2 + (c + dc) % 2
            remote(
                q_in.at[:, rows(p, TD)], qh.at[rows(g, TD), :], sem_send.at[2], sem_q.at[i], p
            ).start()

    frames = frames_ref[...]
    mem = (frames == lax.broadcasted_iota(jnp.int32, (FP, TOK), 0)).astype(f32)
    member[...] = mem.astype(bf16)
    counts = jnp.sum(mem, axis=1, keepdims=True)
    inv_count = jnp.where(counts > 0.0, 1.0 / jnp.maximum(counts, 1.0), 0.0)
    lane_n = lax.broadcasted_iota(jnp.int32, (FP, 128), 1)
    sub_n = lax.broadcasted_iota(jnp.int32, (FP, 128), 0)
    lane_8 = lax.broadcasted_iota(jnp.int32, (16, 128), 1)
    sub_8 = lax.broadcasted_iota(jnp.int32, (16, 128), 0)
    picked = jnp.zeros((FP, 128), f32)
    picked_t = jnp.zeros((16, 128), f32)
    for f in range(FRAMES):
        j = hof_ref[0, f]
        picked = jnp.where((sub_n == f) & (lane_n == j), 1.0, picked)
        picked_t = jnp.where((lane_8 == f) & (sub_8 == j), 1.0, picked_t)
    picked = picked[:, :NDH].astype(bf16)
    picked_t = picked_t[:, :FP].astype(bf16)
    for n in range(DH // 512):
        cols = pl.ds(n * 512, 512)
        part = disc_ref[:, cols]
        total = jnp.zeros((FP, 512), f32)
        for _ in range(3):
            high = part.astype(bf16)
            total = total + mm(picked, high, NN)
            part = part - high.astype(f32)
        head_rows[:, cols] = total

    scale2 = math.log2(math.e) / math.sqrt(HS)
    ck = 512
    bq = 256

    def step(i_s, s_write, i_p, s_read, peak):
        if i_s is not None:
            drain(qh.at[pl.ds(0, bq), :], sem_q.at[i_s])
            qb = qh[rows(q_chip(i_s, -1), bq), :]
            top = jnp.full((bq, 128), -jnp.inf, f32)
        if i_p is not None:
            ch = q_chip(i_p, -1)
            r = rows(ch, bq)
            l = jnp.zeros((bq, 128), f32)
            acc = jnp.zeros((bq, HS), f32)
        for n in range(TOK // ck):
            cols = pl.ds(n * ck, ck)
            if i_s is not None:
                sn = mm(qb, kh[cols, :], NT)
                s_write[:, cols] = sn
                for j in range(ck // 128):
                    top = jnp.maximum(top, sn[:, j * 128:(j + 1) * 128])
            if i_p is not None:
                p = jnp.exp2((s_read[:, cols] - peak) * scale2)
                for j in range(ck // 128):
                    l = l + p[:, j * 128:(j + 1) * 128]
                pb = p.astype(bf16)
                probs[r, cols] = pb
                acc = acc + mm(pb, vh[cols, :], NN)
        if i_p is not None:
            l_col = jnp.sum(l, axis=1, keepdims=True)
            inv = 1.0 / l_col
            oh[r, :] = (acc * inv).astype(bf16)
            inv_row = 1.0 / jnp.sum(jnp.transpose(l), axis=0, keepdims=True)
            wrow[:, r] = inv_row
            memberl[:, r] = (member[:, r].astype(f32) * inv_row).astype(bf16)
            qt = jnp.transpose(qh[r, :].astype(f32))
            qwt[:, r] = (qt * (inv_row * (1.0 / math.sqrt(HS)))).astype(bf16)
            mine = pl.ds(pl.multiple_of(g * HS, HS), HS)
            other = ch * 2 + (1 - c)
            same = ch * 2 + c
            remote(
                oh.at[rows(other, TD), :], lat_out.at[:, mine], sem_send.at[3], sem_recv.at[3], other
            ).start()

            @pl.when(ch != chip)
            def _():
                remote(
                    oh.at[rows(same, TD), :], lat_out.at[:, mine], sem_send.at[3], sem_recv.at[3], same
                ).start()

            @pl.when(ch == chip)
            def _():
                pltpu.make_async_copy(
                    oh.at[rows(same, TD), :], lat_out.at[:, mine], sem_recv.at[3]
                ).start()

        if i_s is not None:
            return jnp.max(top, axis=1, keepdims=True)

    drain(kh, sem_recv.at[0])
    peak0 = step(0, sa, None, None, None)
    drain(vh, sem_recv.at[1])

    @pl.loop(0, 7, init_carry=peak0)
    def fwd(i, peak):
        peak1 = step(2 * i + 1, sb, 2 * i, sa, peak)
        return step(2 * i + 2, sa, 2 * i + 1, sb, peak1)

    peak15 = step(15, sb, 14, sa, fwd)
    step(None, None, 15, sb, peak15)

    pooled = mm(member[...], oh[...], NN) * inv_count
    square = jnp.sum(pooled * pooled, axis=1, keepdims=True)
    pooled_b = pooled.astype(bf16)
    for n in range(DH // 512):
        cols = pl.ds(n * 512, 512)
        rs_src[:, cols] = mm(pooled_b, w_ref[:, cols], NN).astype(bf16)
    lane_o = lax.broadcasted_iota(jnp.int32, (FP, OT), 1)

    def high_low(value):
        high = value.astype(bf16).astype(f32)
        return jnp.where(lane_o == 0, high, jnp.where(lane_o == 1, value - high, 0.0))

    rs_src[:, DH:] = high_low(square).astype(bf16)
    owner = chip + 16 * c

    for off in FAR:
        p = peer(off)
        o = p // 2 + 16 * (p % 2)

        @pl.when(o < OWN)
        def _():
            remote(
                rs_src.at[:, rows(o, OT)], rs_recv.at[rows(g, FP), :],
                sem_send.at[4], sem_recv.at[4], p,
            ).start()

    @pl.when(owner < OWN)
    def _():
        pltpu.make_async_copy(
            rs_src.at[:, rows(owner, OT)], rs_recv.at[rows(g, FP), :], sem_recv.at[4]
        ).start()

    def frame_sums(lo, hi):
        for n in range(lo, hi):
            cols = pl.ds(n * 512, 512)
            rbuf[:, cols] = mm(memberl[...], probs[:, cols], NN).astype(bf16)

    frame_sums(0, 3)

    @pl.when(owner < OWN)
    def _():
        drain(rs_recv, sem_recv.at[4])
        total = jnp.zeros((FP, OT), f32)
        for n in range(GEN):
            total = total + rs_recv[n * FP:(n + 1) * FP, :].astype(f32)
        both = high_low(total[:, 0:1] + total[:, 1:2])
        total = jnp.where(owner == OWN - 1, both, total)
        ag_src[...] = total.astype(bf16)
        pltpu.make_async_copy(ag_src, proj.at[:, rows(owner, OT)], sem_recv.at[5]).start()
        for off in FAR:
            p = peer(off)
            remote(
                ag_src, proj.at[:, rows(owner, OT)], sem_send.at[5], sem_recv.at[5], p
            ).start()

    frame_sums(3, 8)
    pltpu.make_async_copy(rbuf.at[:, rows(g, TD)], r_all.at[rows(g, FP), :], sem_recv.at[6]).start()
    for off in FAR:
        p = peer(off)
        remote(
            rbuf.at[:, rows(p, TD)], r_all.at[rows(g, FP), :], sem_send.at[6], sem_recv.at[6], p
        ).start()
    drain(proj, sem_recv.at[5])

    squares = proj[:, DH:DH + 128].astype(f32)
    squares = squares[:, 0:1] + squares[:, 1:2]
    root = jnp.sqrt(squares / (GEN * HS) + EPS)
    score = jnp.zeros((FP, 1), f32)
    for n in range(DH // 512):
        cols = pl.ds(n * 512, 512)
        pre = proj[:, cols].astype(f32) / root
        feature = pre * jax.nn.sigmoid(pre)
        gsf[:, cols] = feature
        score = score + jnp.sum(feature * head_rows[:, cols], axis=1, keepdims=True)
    weight = (time_ref[0].astype(f32) + 1.0) / NSTEPS
    grad_score = -weight * jax.nn.sigmoid(-score) / FRAMES
    dot_sum = jnp.zeros((FP, 1), f32)
    grad_pooled = jnp.zeros((FP, HS), f32)
    for n in range(DH // 512):
        cols = pl.ds(n * 512, 512)
        pre = proj[:, cols].astype(f32) / root
        gate = jax.nn.sigmoid(pre)
        grad_pre = grad_score * head_rows[:, cols] * gate * (1.0 + pre * (1.0 - gate))
        dot_sum = dot_sum + jnp.sum(grad_pre * pre, axis=1, keepdims=True)
        grad_pooled = grad_pooled + mm((grad_pre / root).astype(bf16), w_ref[:, cols], NT)
    grad_root = -dot_sum / root
    grad_pooled = grad_pooled + (grad_root / root / (GEN * HS)) * pooled
    table = (TOK * (grad_pooled * inv_count)).astype(bf16)
    g_src[...] = table
    pltpu.make_async_copy(g_src, g_all.at[rows(g, FP), :], sem_recv.at[7]).start()
    for off in FAR:
        p = peer(off)
        remote(g_src, g_all.at[rows(g, FP), :], sem_send.at[7], sem_recv.at[7], p).start()

    for n in range(DH // 512):
        cols = pl.ds(n * 512, 512)
        value = grad_score * gsf[:, cols]
        high = value.astype(bf16)
        low = (value - high.astype(f32)).astype(bf16)
        hp_src[:, cols] = (mm(picked_t, high, NN) + mm(picked_t, low, NN)).astype(bf16)
    pltpu.make_async_copy(hp_src, hp_all.at[rows(x, 16), :], sem_recv.at[8]).start()
    for d in range(1, GRP):
        pltpu.make_async_remote_copy(
            src_ref=hp_src, dst_ref=hp_all.at[rows(x, 16), :],
            send_sem=sem_send.at[8], recv_sem=sem_recv.at[8],
            device_id={"grp": (x + d) % GRP}, device_id_type=MESH,
        ).start()

    bt = 512
    cb = 1024
    dkt[...] = jnp.zeros_like(dkt)
    mine = pl.ds(pl.multiple_of(g * HS, HS), HS)

    @pl.loop(0, TOK // bt)
    def _(i):
        blk = (i + g // 4) % (TOK // bt)
        r = rows(blk, bt)
        grad_rows = mm(member[:, r], g_src[...], TN)
        delta = jnp.sum(grad_rows * oh[r, :].astype(f32), axis=1, keepdims=True)
        grad_b = grad_rows.astype(bf16)
        acc = jnp.zeros((bt, HS), f32)
        qb = qwt[:, r]
        for n in range(TOK // cb):
            cols = pl.ds(n * cb, cb)
            dp = mm(grad_b, vh[cols, :], NT)
            ds = (dp - delta).astype(bf16) * probs[r, cols]
            acc = acc + mm(ds, kh[cols, :], NN)
            dkt[:, cols] += mm(qb, ds, NN)
        w_cols = jnp.transpose(jnp.broadcast_to(wrow[:, r] * (1.0 / math.sqrt(HS)), (HS, bt)))
        qh[r, :] = (acc * w_cols).astype(bf16)
        for d in range(bt // TD):
            p = blk * (bt // TD) + d

            @pl.when(p != g)
            def _():
                remote(
                    qh.at[rows(p, TD), :], dq_out.at[:, mine], sem_send.at[9], sem_recv.at[9], p
                ).start()

            @pl.when(p == g)
            def _():
                pltpu.make_async_copy(
                    qh.at[rows(p, TD), :], dq_out.at[:, mine], sem_recv.at[9]
                ).start()

    for off in FAR + [None]:
        p = g if off is None else peer(off)
        kh[rows(p, TD), :] = jnp.transpose(dkt[:, rows(p, TD)]).astype(bf16)
        if off is None:
            pltpu.make_async_copy(kh.at[rows(p, TD), :], dk_out.at[:, mine], sem_recv.at[10]).start()
        else:
            remote(
                kh.at[rows(p, TD), :], dk_out.at[:, mine], sem_send.at[10], sem_recv.at[10], p
            ).start()

    drain(r_all, sem_recv.at[6])
    drain(g_all, sem_recv.at[7])
    for h in range(GEN):
        hr = pl.ds(h * FP, FP)
        dv_out[:, h * HS:(h + 1) * HS] = mm(r_all[hr, :], g_all[hr, :], TN).astype(bf16)
    drain(hp_all, sem_recv.at[8])
    total = jnp.zeros((16, DH), f32)
    for n in range(GRP):
        total = total + hp_all[n * 16:(n + 1) * 16, :].astype(f32)
    gh_out[...] = total[:NDH, :]

    drain(lat_out, sem_recv.at[3])
    drain(dq_out, sem_recv.at[9])
    drain(dk_out, sem_recv.at[10])
    sent = kh.at[pl.ds(0, (GEN - 1) * TD), :]
    for n in (0, 1, 2, 3, 9, 10):
        drain(sent, sem_send.at[n])

    @pl.when(owner < OWN)
    def _():
        drain(rs_src.at[:, pl.ds(0, (OWN - 1) * OT)], sem_send.at[4])
        drain(rs_recv.at[pl.ds(0, (GEN - 1) * FP), :], sem_send.at[5])

    @pl.when(owner >= OWN)
    def _():
        drain(rs_src, sem_send.at[4])

    drain(r_all.at[pl.ds(0, (GEN - 1) * FP), :], sem_send.at[6])
    drain(g_all.at[pl.ds(0, (GEN - 1) * FP), :], sem_send.at[7])
    drain(hp_all.at[pl.ds(0, (GRP - 1) * 16), :], sem_send.at[8])


def on_device(
    query_in, key_in, value_in, teacher_w, disc_heads, frame_of_token, head_of_frame, timestep
):
    vmem = pl.BlockSpec(memory_space=pltpu.VMEM)
    smem = pl.BlockSpec(memory_space=pltpu.SMEM)
    hbm = pl.BlockSpec(memory_space=pl.ANY)
    rows_shape = jax.ShapeDtypeStruct((TD, GEN * HS), bf16)
    V = pltpu.VMEM
    outs = pl.pallas_call(
        body,
        out_shape=(
            rows_shape, rows_shape, rows_shape, rows_shape,
            jax.ShapeDtypeStruct((NDH, DH), f32),
        ),
        in_specs=[hbm, hbm, hbm, vmem, vmem, vmem, smem, smem],
        out_specs=(hbm, hbm, hbm, vmem, vmem),
        scratch_shapes=[
            V((TOK, TOK), bf16),
            V((TOK, HS), bf16), V((TOK, HS), bf16), V((TOK, HS), bf16), V((TOK, HS), bf16),
            V((256, TOK), f32), V((256, TOK), f32),
            V((HS, TOK), f32), V((HS, TOK), bf16), V((1, TOK), f32),
            V((FP, TOK), bf16), V((FP, TOK), bf16), V((FP, TOK), bf16),
            V((GEN * FP, TD), bf16), V((FP, HS), bf16), V((GEN * FP, HS), bf16),
            V((FP, DH + OT), bf16), V((GEN * FP, OT), bf16), V((FP, OT), bf16),
            V((FP, DH + OT), bf16), V((FP, DH), f32), V((FP, DH), f32),
            V((16, DH), bf16), V((GRP * 16, DH), bf16),
            pltpu.SemaphoreType.DMA((11,)),
            pltpu.SemaphoreType.DMA((16,)),
            pltpu.SemaphoreType.DMA((11,)),
        ],
        compiler_params=pltpu.CompilerParams(
            collective_id=0, has_side_effects=True, vmem_limit_bytes=63 * 1024 * 1024
        ),
        name="clip_step",
    )(
        query_in[0], key_in[0], value_in[0], teacher_w, disc_heads,
        frame_of_token, head_of_frame, timestep,
    )
    lat, dq, dk, dv, gh = outs
    return (lat[None], dq[None], dk[None], dv[None], gh)


def solution(mesh):
    return jax.shard_map(
        on_device,
        mesh=mesh,
        in_specs=(
            P("grp", "gen", None),
            P("grp", "gen", None),
            P("grp", "gen", None),
            P("gen", None),
            P(),
            P("grp", None),
            P("grp", None),
            P("grp"),
        ),
        out_specs=(
            P("grp", "gen", None),
            P("grp", "gen", None),
            P("grp", "gen", None),
            P("grp", "gen", None),
            P(),
        ),
        check_vma=False,
    )
```

time: 555 us -> 142 us (0.26)
  waiting for transfers between devices: 209 us -> 0 us
  matrix products: 144 us -> 0 us
  Pallas kernels: 0 us -> 133 us
  blocking collectives: 69.7 us -> 0 us
  local copies, waits for them, and re-layouts: 52.8 us -> 7.31 us
  starting transfers between devices: 37.4 us -> 0 us
  other arithmetic: 23.3 us -> 0 us
  between operations: 14.9 us -> 1.3 us
    dot_general x61 -> x0, matrix products: 144 us -> none  [the longest x8 29 us: backward_rows(): jnp.einsum('rhd,thd->hrt', grad_rows, value_three, preferred_element_type...]
    psum x2 -> x0, waiting for transfers between devices: 138 us -> none  [the longest x1 97.3 us: on_device(): lax.psum(project_part.astype(jnp.bfloat16), 'gen').astype(jnp.float32)]
    pallas_call x0 -> x1, Pallas kernels: none -> 133 us  [on_device(): pl.pallas_call(body, out_shape=(rows_shape, rows_shape, rows_shape, rows_...]
    all_to_all x7 -> x0, waiting for transfers between devices: 70.9 us -> none  [the longest x1 15.6 us: on_device(): lax.all_to_all(seq_rows[0], 'gen', split_axis=1, concat_axis=0, tiled=True)]
    psum x1 -> x0, blocking collectives: 69.7 us -> none  [on_device(): lax.psum(square_part.astype(jnp.bfloat16), 'gen').astype(jnp.float32)]
    all_to_all x7 -> x0, starting transfers between devices: 37.1 us -> none  [the longest x1 9.6 us: on_device(): lax.all_to_all(seq_rows[0], 'gen', split_axis=1, concat_axis=0, tiled=True)]
    reduce_sum x11 -> x0, other arithmetic: 15.5 us -> none  [the longest x8 12.1 us: forward_rows(): total = jnp.sum(weights, axis=2, keepdims=True)]
    gather x1 -> x0, local copies, waits for them, and re-layouts: 14.1 us -> none  [on_device(): jnp.take(spread, frames, axis=0)]
  transfers between devices with their start and end apart: 9 -> 0, of which waited for: 7 -> 0; matrix products, arithmetic and copies ran while one was open for 28% -> 0% of each run, Pallas kernels for 0% -> 0%
where the time goes in v1:
time: 142 us
  Pallas kernels  133 us (94%)
  local copies, waits for them, and re-layouts  7.31 us (5%)
    pallas_call x1, Pallas kernels, on_device(): pl.pallas_call(body, out_shape=(rows_shape, rows_shape, rows_shape, rows_...  133 us
    unnamed x13, local copies, waits for them, and re-layouts  7.31 us

profile of v1, /device:TPU:1, one launch (start us, length us, event | category | flops | bytes accessed | tf_op | source)
XLA Modules:
  0.0 141.8 jit_solution(4733684998025031729)
XLA Ops:
  1.3 133.2 %clip_step.1 = (bf16[128,4096]{1,0:T(8,128)(2,1)}, bf16[128,4096]{1,0:T(8,128)(2,1)}, bf16[128,4096]{1,0:T(8,128)(2,1)}, bf16[128,4096]{1,0:T(8,128)(2,1)}, f32[8,5120]{1,0:T(8,128)}) custom-call(bf16[128,4096]{1,0:T(8,128)(2,1)} %bitcast.7, bf16[128,4096]{1,0:T(8,128)(2,1)} %bitcast.8, bf16[128,4096]{1,0:T(8,128)(2,1)} %bitcast.9, bf16[128,5120]{1,0:T(8,128)(2,1)} %w_ref.1, ...), custom_call_target="tpu_custom_call" | custom-call | tf_op jit(solution)/shard_map/clip_step/pallas_call | solution.py:399
  134.5 0.0 copy-start.2
  134.5 2.4 %copy.19 = bf16[1,128,4096]{2,1,0:T(8,128)(2,1)} copy(bf16[1,128,4096]{2,1,0:T(8,128)(2,1)} %bitcast.13) | data formatting | bytes 2097152
  136.8 0.0 copy-done.2
  136.8 0.0 copy-start.1
  136.8 1.0 copy.20
  137.8 0.6 copy-done.1
  138.4 0.0 copy-start
  138.4 1.0 copy.21
  139.4 0.6 copy-done
  140.0 0.0 copy-start.3
  140.1 1.0 copy.22
  141.0 0.1 copy-done.3
  141.1 0.7 copy.23
Async XLA Ops:
  134.5 2.4 %copy-start.2 = (bf16[128,4096]{1,0:T(8,128)(2,1)S(1)}, bf16[128,4096]{1,0:T(8,128)(2,1)}, u32[]{:S(2)}) copy-start(bf16[128,4096]{1,0:T(8,128)(2,1)} %get-tuple-element.11) | copy-start | bytes 3145732
  136.8 1.6 %copy-start.1 = (bf16[128,4096]{1,0:T(8,128)(2,1)S(1)}, bf16[128,4096]{1,0:T(8,128)(2,1)}, u32[]{:S(2)}) copy-start(bf16[128,4096]{1,0:T(8,128)(2,1)} %get-tuple-element.12) | copy-start | bytes 3145732
  138.4 1.6 %copy-start = (bf16[128,4096]{1,0:T(8,128)(2,1)S(1)}, bf16[128,4096]{1,0:T(8,128)(2,1)}, u32[]{:S(2)}) copy-start(bf16[128,4096]{1,0:T(8,128)(2,1)} %get-tuple-element.13) | copy-start | bytes 3145732
  140.0 1.1 copy-start.3

commit v2 on v1

--- a/solution.py
+++ b/solution.py
@@ -42,7 +42,7 @@
     q_in, k_in, v_in, w_ref, disc_ref, frames_ref, hof_ref, time_ref,
     lat_out, dq_out, dk_out, dv_out, gh_out,
     probs, qh, kh, vh, oh, sa, sb, dkt, qwt, wrow, member, memberl, rbuf, r_all, g_src, g_all,
-    rs_src, rs_recv, ag_src, proj, head_rows, gsf, hp_src, hp_all,
+    rs_src, rs_recv, ag_src, proj, head_rows, gsf, hp_src, hp_all, dob,
     sem_send, sem_q, sem_recv,
 ):
     g = lax.axis_index("gen")
@@ -139,6 +139,7 @@
             drain(qh.at[pl.ds(0, bq), :], sem_q.at[i_s])
             qb = qh[rows(q_chip(i_s, -1), bq), :]
             top = jnp.full((bq, 128), -jnp.inf, f32)
+            qwt[:, rows(q_chip(i_s, -1), bq)] = jnp.transpose(qb.astype(f32)).astype(bf16)
         if i_p is not None:
             ch = q_chip(i_p, -1)
             r = rows(ch, bq)
@@ -162,11 +163,7 @@
             l_col = jnp.sum(l, axis=1, keepdims=True)
             inv = 1.0 / l_col
             oh[r, :] = (acc * inv).astype(bf16)
-            inv_row = 1.0 / jnp.sum(jnp.transpose(l), axis=0, keepdims=True)
-            wrow[:, r] = inv_row
-            memberl[:, r] = (member[:, r].astype(f32) * inv_row).astype(bf16)
-            qt = jnp.transpose(qh[r, :].astype(f32))
-            qwt[:, r] = (qt * (inv_row * (1.0 / math.sqrt(HS)))).astype(bf16)
+            wrow[:, r] = 1.0 / jnp.sum(jnp.transpose(l), axis=0, keepdims=True)
             mine = pl.ds(pl.multiple_of(g * HS, HS), HS)
             other = ch * 2 + (1 - c)
             same = ch * 2 + c
@@ -238,7 +235,8 @@
             cols = pl.ds(n * 512, 512)
             rbuf[:, cols] = mm(memberl[...], probs[:, cols], NN).astype(bf16)
 
-    frame_sums(0, 3)
+    memberl[...] = (member[...].astype(f32) * wrow[...]).astype(bf16)
+    frame_sums(0, 4)
 
     @pl.when(owner < OWN)
     def _():
@@ -256,7 +254,7 @@
                 ag_src, proj.at[:, rows(owner, OT)], sem_send.at[5], sem_recv.at[5], p
             ).start()
 
-    frame_sums(3, 8)
+    frame_sums(4, 8)
     pltpu.make_async_copy(rbuf.at[:, rows(g, TD)], r_all.at[rows(g, FP), :], sem_recv.at[6]).start()
     for off in FAR:
         p = peer(off)
@@ -268,32 +266,127 @@
     squares = proj[:, DH:DH + 128].astype(f32)
     squares = squares[:, 0:1] + squares[:, 1:2]
     root = jnp.sqrt(squares / (GEN * HS) + EPS)
+    inv_root = 1.0 / root
     score = jnp.zeros((FP, 1), f32)
+    dot_sum = jnp.zeros((FP, 1), f32)
+    raw = jnp.zeros((FP, HS), f32)
     for n in range(DH // 512):
         cols = pl.ds(n * 512, 512)
-        pre = proj[:, cols].astype(f32) / root
-        feature = pre * jax.nn.sigmoid(pre)
+        hr = head_rows[:, cols]
+        pre = proj[:, cols].astype(f32) * inv_root
+        gate = jax.nn.sigmoid(pre)
+        feature = pre * gate
         gsf[:, cols] = feature
-        score = score + jnp.sum(feature * head_rows[:, cols], axis=1, keepdims=True)
+        slope = hr * (gate + feature * (1.0 - gate))
+        score = score + jnp.sum(feature * hr, axis=1, keepdims=True)
+        dot_sum = dot_sum + jnp.sum(slope * pre, axis=1, keepdims=True)
+        raw = raw + mm(slope.astype(bf16), w_ref[:, cols], NT)
     weight = (time_ref[0].astype(f32) + 1.0) / NSTEPS
     grad_score = -weight * jax.nn.sigmoid(-score) / FRAMES
-    dot_sum = jnp.zeros((FP, 1), f32)
-    grad_pooled = jnp.zeros((FP, HS), f32)
-    for n in range(DH // 512):
-        cols = pl.ds(n * 512, 512)
-        pre = proj[:, cols].astype(f32) / root
-        gate = jax.nn.sigmoid(pre)
-        grad_pre = grad_score * head_rows[:, cols] * gate * (1.0 + pre * (1.0 - gate))
-        dot_sum = dot_sum + jnp.sum(grad_pre * pre, axis=1, keepdims=True)
-        grad_pooled = grad_pooled + mm((grad_pre / root).astype(bf16), w_ref[:, cols], NT)
-    grad_root = -dot_sum / root
-    grad_pooled = grad_pooled + (grad_root / root / (GEN * HS)) * pooled
+    grad_pooled = (grad_score * inv_root) * raw
+    grad_pooled = grad_pooled - (grad_score * dot_sum * inv_root * inv_root / (GEN * HS)) * pooled
     table = (TOK * (grad_pooled * inv_count)).astype(bf16)
     g_src[...] = table
     pltpu.make_async_copy(g_src, g_all.at[rows(g, FP), :], sem_recv.at[7]).start()
     for off in FAR:
         p = peer(off)
         remote(g_src, g_all.at[rows(g, FP), :], sem_send.at[7], sem_recv.at[7], p).start()
+
+    bt = 512
+    half = TOK // bt // 2
+    cb = 1024
+    inv_scale = 1.0 / math.sqrt(HS)
+    mine = pl.ds(pl.multiple_of(g * HS, HS), HS)
+    spin = g // 4
+
+    def give(src, p, out, which):
+        @pl.when(p != g)
+        def _():
+            remote(
+                src.at[rows(p, TD), :], out.at[:, mine], sem_send.at[which], sem_recv.at[which], p
+            ).start()
+
+        @pl.when(p == g)
+        def _():
+            pltpu.make_async_copy(
+                src.at[rows(p, TD), :], out.at[:, mine], sem_recv.at[which]
+            ).start()
+
+    def block_of(i):
+        return (i + spin) % (TOK // bt)
+
+    def grads_of(r):
+        grad_rows = mm(member[:, r], g_src[...], TN)
+        delta = jnp.sum(grad_rows * oh[r, :].astype(f32), axis=1, keepdims=True)
+        return grad_rows.astype(bf16), delta
+
+    def scaled_q(r):
+        return (qwt[:, r].astype(f32) * (wrow[:, r] * inv_scale)).astype(bf16)
+
+    def finish_q(r, acc):
+        w_cols = jnp.transpose(jnp.broadcast_to(wrow[:, r] * inv_scale, (HS, bt)))
+        qh[r, :] = (acc * w_cols).astype(bf16)
+
+    def part(j, k):
+        return pl.ds((2 * j + k) * HS, HS)
+
+    def store_part(ref, j, value):
+        ref[:, part(j, 0)] = value[:bq, :]
+        ref[:, part(j, 1)] = value[bq:, :]
+
+    def load_part(ref, j):
+        return jnp.concatenate([ref[:, part(j, 0)], ref[:, part(j, 1)]], axis=0)
+
+    dkt[...] = jnp.zeros_like(dkt)
+
+    @pl.loop(0, half)
+    def _(i):
+        blk = block_of(i)
+        r = rows(blk, bt)
+        grad_b, delta = grads_of(r)
+        acc = jnp.zeros((bt, HS), f32)
+        qb = scaled_q(r)
+        for n in range(TOK // cb):
+            cols = pl.ds(n * cb, cb)
+            dp = mm(grad_b, vh[cols, :], NT)
+            ds = (dp - delta).astype(bf16) * probs[r, cols]
+            acc = acc + mm(ds, kh[cols, :], NN)
+            dkt[:, cols] += mm(qb, ds, NN)
+        finish_q(r, acc)
+        for d in range(bt // TD):
+            give(qh, blk * (bt // TD) + d, dq_out, 9)
+
+    for j in range(half):
+        r = rows(block_of(half + j), bt)
+        grad_b, delta = grads_of(r)
+        dob[j * bt:(j + 1) * bt, :] = grad_b
+        store_part(sb, j, jnp.broadcast_to(delta, (bt, HS)))
+        store_part(sa, j, jnp.zeros((bt, HS), f32))
+        qwt[:, r] = scaled_q(r)
+
+    @pl.loop(0, TOK // bt)
+    def _(i):
+        blk = block_of(i)
+        cols = rows(blk, bt)
+        kc = kh[cols, :]
+        vc = vh[cols, :]
+        dk = dkt[:, cols]
+        for j in range(half):
+            r = rows(block_of(half + j), bt)
+            jr = slice(j * bt, (j + 1) * bt)
+            dp = mm(dob[jr, :], vc, NT)
+            ds = (dp - load_part(sb, j)[:, 0:1]).astype(bf16) * probs[r, cols]
+            store_part(sa, j, load_part(sa, j) + mm(ds, kc, NN))
+            dk = dk + mm(qwt[:, r], ds, NN)
+        kh[cols, :] = jnp.transpose(dk).astype(bf16)
+        for d in range(bt // TD):
+            give(kh, blk * (bt // TD) + d, dk_out, 10)
+
+    for j in range(half):
+        blk = block_of(half + j)
+        finish_q(rows(blk, bt), load_part(sa, j))
+        for d in range(bt // TD):
+            give(qh, blk * (bt // TD) + d, dq_out, 9)
 
     for n in range(DH // 512):
         cols = pl.ds(n * 512, 512)
@@ -309,64 +402,20 @@
             device_id={"grp": (x + d) % GRP}, device_id_type=MESH,
         ).start()
 
-    bt = 512
-    cb = 1024
-    dkt[...] = jnp.zeros_like(dkt)
-    mine = pl.ds(pl.multiple_of(g * HS, HS), HS)
-
-    @pl.loop(0, TOK // bt)
-    def _(i):
-        blk = (i + g // 4) % (TOK // bt)
-        r = rows(blk, bt)
-        grad_rows = mm(member[:, r], g_src[...], TN)
-        delta = jnp.sum(grad_rows * oh[r, :].astype(f32), axis=1, keepdims=True)
-        grad_b = grad_rows.astype(bf16)
-        acc = jnp.zeros((bt, HS), f32)
-        qb = qwt[:, r]
-        for n in range(TOK // cb):
-            cols = pl.ds(n * cb, cb)
-            dp = mm(grad_b, vh[cols, :], NT)
-            ds = (dp - delta).astype(bf16) * probs[r, cols]
-            acc = acc + mm(ds, kh[cols, :], NN)
-            dkt[:, cols] += mm(qb, ds, NN)
-        w_cols = jnp.transpose(jnp.broadcast_to(wrow[:, r] * (1.0 / math.sqrt(HS)), (HS, bt)))
-        qh[r, :] = (acc * w_cols).astype(bf16)
-        for d in range(bt // TD):
-            p = blk * (bt // TD) + d
-
-            @pl.when(p != g)
-            def _():
-                remote(
-                    qh.at[rows(p, TD), :], dq_out.at[:, mine], sem_send.at[9], sem_recv.at[9], p
-                ).start()
-
-            @pl.when(p == g)
-            def _():
-                pltpu.make_async_copy(
-                    qh.at[rows(p, TD), :], dq_out.at[:, mine], sem_recv.at[9]
-                ).start()
-
-    for off in FAR + [None]:
-        p = g if off is None else peer(off)
-        kh[rows(p, TD), :] = jnp.transpose(dkt[:, rows(p, TD)]).astype(bf16)
-        if off is None:
-            pltpu.make_async_copy(kh.at[rows(p, TD), :], dk_out.at[:, mine], sem_recv.at[10]).start()
-        else:
-            remote(
-                kh.at[rows(p, TD), :], dk_out.at[:, mine], sem_send.at[10], sem_recv.at[10], p
-            ).start()
-
     drain(r_all, sem_recv.at[6])
     drain(g_all, sem_recv.at[7])
     for h in range(GEN):
         hr = pl.ds(h * FP, FP)
-        dv_out[:, h * HS:(h + 1) * HS] = mm(r_all[hr, :], g_all[hr, :], TN).astype(bf16)
+        qwt[:, h * HS:(h + 1) * HS] = mm(r_all[hr, :], g_all[hr, :], TN).astype(bf16)
+    to_dv = pltpu.make_async_copy(qwt, dv_out, sem_recv.at[1])
+    to_dv.start()
     drain(hp_all, sem_recv.at[8])
     total = jnp.zeros((16, DH), f32)
     for n in range(GRP):
         total = total + hp_all[n * 16:(n + 1) * 16, :].astype(f32)
     gh_out[...] = total[:NDH, :]
 
+    to_dv.wait()
     drain(lat_out, sem_recv.at[3])
     drain(dq_out, sem_recv.at[9])
     drain(dk_out, sem_recv.at[10])
@@ -386,6 +435,22 @@
     drain(r_all.at[pl.ds(0, (GEN - 1) * FP), :], sem_send.at[6])
     drain(g_all.at[pl.ds(0, (GEN - 1) * FP), :], sem_send.at[7])
     drain(hp_all.at[pl.ds(0, (GRP - 1) * 16), :], sem_send.at[8])
+
+
+def settle(*refs):
+    sem = refs[-1]
+    n = (len(refs) - 1) // 2
+    copies = []
+    for i in range(n):
+        parts = 4 if i < n - 1 else 1
+        step = refs[i].shape[0] // parts
+        for j in range(parts):
+            r = pl.ds(j * step, step)
+            copy = pltpu.make_async_copy(refs[i].at[r], refs[n + i].at[r], sem.at[len(copies)])
+            copy.start()
+            copies.append(copy)
+    for copy in copies:
+        copy.wait()
 
 
 def on_device(
@@ -403,7 +468,7 @@
             jax.ShapeDtypeStruct((NDH, DH), f32),
         ),
         in_specs=[hbm, hbm, hbm, vmem, vmem, vmem, smem, smem],
-        out_specs=(hbm, hbm, hbm, vmem, vmem),
+        out_specs=(hbm, hbm, hbm, hbm, vmem),
         scratch_shapes=[
             V((TOK, TOK), bf16),
             V((TOK, HS), bf16), V((TOK, HS), bf16), V((TOK, HS), bf16), V((TOK, HS), bf16),
@@ -414,6 +479,7 @@
             V((FP, DH + OT), bf16), V((GEN * FP, OT), bf16), V((FP, OT), bf16),
             V((FP, DH + OT), bf16), V((FP, DH), f32), V((FP, DH), f32),
             V((16, DH), bf16), V((GRP * 16, DH), bf16),
+            V((TOK // 2, HS), bf16),
             pltpu.SemaphoreType.DMA((11,)),
             pltpu.SemaphoreType.DMA((16,)),
             pltpu.SemaphoreType.DMA((11,)),
@@ -426,7 +492,14 @@
         query_in[0], key_in[0], value_in[0], teacher_w, disc_heads,
         frame_of_token, head_of_frame, timestep,
     )
-    lat, dq, dk, dv, gh = outs
+    lat, dq, dk, dv, gh = pl.pallas_call(
+        settle,
+        out_shape=tuple(jax.ShapeDtypeStruct(o.shape, o.dtype) for o in outs),
+        in_specs=[hbm] * 5,
+        out_specs=(hbm,) * 5,
+        scratch_shapes=[pltpu.SemaphoreType.DMA((17,))],
+        name="settle",
+    )(*outs)
     return (lat[None], dq[None], dk[None], dv[None], gh)
 
 

time: 142 us -> 268 us (1.89)
  Pallas kernels: 133 us -> 266 us
  local copies, waits for them, and re-layouts: 7.31 us -> 0 us
    pallas_call x0 -> x1, Pallas kernels: none -> 133 us  [on_device(): pl.pallas_call(settle, out_shape=tuple((jax.ShapeDtypeStruct(o.shape, o.d...]
    unnamed x13 -> x0, local copies, waits for them, and re-layouts: 7.31 us -> none
where the time goes in v2:
time: 268 us; the launch traced here: 267 us
  Pallas kernels  266 us (99%)
    pallas_call x1, Pallas kernels, on_device(): pl.pallas_call(settle, out_shape=tuple((jax.ShapeDtypeStruct(o.shape, o.d...  133 us
    pallas_call x1, Pallas kernels, on_device(): pl.pallas_call(body, out_shape=(rows_shape, rows_shape, rows_shape, rows_...  133 us

profile of v2, /device:TPU:1, one launch (start us, length us, event | category | flops | bytes accessed | tf_op | source)
XLA Modules:
  0.0 267.4 jit_solution(187176247010889631)
XLA Ops:
  1.3 132.7 %clip_step.1 = (bf16[128,4096]{1,0:T(8,128)(2,1)}, bf16[128,4096]{1,0:T(8,128)(2,1)}, bf16[128,4096]{1,0:T(8,128)(2,1)}, bf16[128,4096]{1,0:T(8,128)(2,1)}, f32[8,5120]{1,0:T(8,128)}) custom-call(bf16[128,4096]{1,0:T(8,128)(2,1)} %bitcast.7, bf16[128,4096]{1,0:T(8,128)(2,1)} %bitcast.8, bf16[128,4096]{1,0:T(8,128)(2,1)} %bitcast.9, bf16[128,5120]{1,0:T(8,128)(2,1)} %w_ref.1, ...), custom_call_target="tpu_custom_call" | custom-call | tf_op jit(solution)/shard_map/clip_step/pallas_call | solution.py:464
  134.0 133.3 %settle.1 = (bf16[128,4096]{1,0:T(8,128)(2,1)}, bf16[128,4096]{1,0:T(8,128)(2,1)}, bf16[128,4096]{1,0:T(8,128)(2,1)}, bf16[128,4096]{1,0:T(8,128)(2,1)}, f32[8,5120]{1,0:T(8,128)}) custom-call(bf16[128,4096]{1,0:T(8,128)(2,1)} %get-tuple-element.15.refs_0_, bf16[128,4096]{1,0:T(8,128)(2,1)} %get-tuple-element.16.refs_1_, ...), custom_call_target="tpu_custom_call" | custom-call | tf_op jit(solution)/shard_map/settle/pallas_call | solution.py:495

commit v3 on v2

--- a/solution.py
+++ b/solution.py
@@ -42,7 +42,7 @@
     q_in, k_in, v_in, w_ref, disc_ref, frames_ref, hof_ref, time_ref,
     lat_out, dq_out, dk_out, dv_out, gh_out,
     probs, qh, kh, vh, oh, sa, sb, dkt, qwt, wrow, member, memberl, rbuf, r_all, g_src, g_all,
-    rs_src, rs_recv, ag_src, proj, head_rows, gsf, hp_src, hp_all, dob,
+    rs_src, rs_recv, ag_src, proj, head_rows, gsf, hp_src, hp_all,
     sem_send, sem_q, sem_recv,
 ):
     g = lax.axis_index("gen")
@@ -79,8 +79,15 @@
         )
     pl.semaphore_wait(barrier, GEN - 1 + GRP - 1)
 
-    for src, dst, which in ((k_in, kh, 0), (v_in, vh, 1)):
-        pltpu.make_async_copy(src.at[:, rows(g, TD)], dst.at[rows(g, TD), :], sem_recv.at[which]).start()
+    def q_chip(i, sign):
+        dy = i % 4
+        dz = (i // 4 + i) % 4
+        return ((y + sign * dy + 4) % 4) * 4 + (z + sign * dz + 4) % 4
+
+    def gather_rows(src, dst, which):
+        pltpu.make_async_copy(
+            src.at[:, rows(g, TD)], dst.at[rows(g, TD), :], sem_recv.at[which]
+        ).start()
         for off in FAR:
             p = peer(off)
             remote(
@@ -88,11 +95,7 @@
                 sem_send.at[which], sem_recv.at[which], p,
             ).start()
 
-    def q_chip(i, sign):
-        dy = i % 4
-        dz = (i // 4 + i) % 4
-        return ((y + sign * dy + 4) % 4) * 4 + (z + sign * dz + 4) % 4
-
+    gather_rows(k_in, kh, 0)
     pltpu.make_async_copy(q_in.at[:, rows(g, TD)], qh.at[rows(g, TD), :], sem_q.at[0]).start()
     for i in range(16):
         for dc in (0, 1):
@@ -102,6 +105,7 @@
             remote(
                 q_in.at[:, rows(p, TD)], qh.at[rows(g, TD), :], sem_send.at[2], sem_q.at[i], p
             ).start()
+    gather_rows(v_in, vh, 1)
 
     frames = frames_ref[...]
     mem = (frames == lax.broadcasted_iota(jnp.int32, (FP, TOK), 0)).astype(f32)
@@ -137,14 +141,13 @@
     def step(i_s, s_write, i_p, s_read, peak):
         if i_s is not None:
             drain(qh.at[pl.ds(0, bq), :], sem_q.at[i_s])
-            qb = qh[rows(q_chip(i_s, -1), bq), :]
+            rs = rows(q_chip(i_s, -1), bq)
+            qb = qh[rs, :]
             top = jnp.full((bq, 128), -jnp.inf, f32)
-            qwt[:, rows(q_chip(i_s, -1), bq)] = jnp.transpose(qb.astype(f32)).astype(bf16)
+            qwt[:, rs] = jnp.transpose(qb.astype(f32)).astype(bf16)
         if i_p is not None:
-            ch = q_chip(i_p, -1)
-            r = rows(ch, bq)
+            r = rows(q_chip(i_p, -1), bq)
             l = jnp.zeros((bq, 128), f32)
-            acc = jnp.zeros((bq, HS), f32)
         for n in range(TOK // ck):
             cols = pl.ds(n * ck, ck)
             if i_s is not None:
@@ -156,39 +159,14 @@
                 p = jnp.exp2((s_read[:, cols] - peak) * scale2)
                 for j in range(ck // 128):
                     l = l + p[:, j * 128:(j + 1) * 128]
-                pb = p.astype(bf16)
-                probs[r, cols] = pb
-                acc = acc + mm(pb, vh[cols, :], NN)
+                probs[r, cols] = p.astype(bf16)
         if i_p is not None:
-            l_col = jnp.sum(l, axis=1, keepdims=True)
-            inv = 1.0 / l_col
-            oh[r, :] = (acc * inv).astype(bf16)
             wrow[:, r] = 1.0 / jnp.sum(jnp.transpose(l), axis=0, keepdims=True)
-            mine = pl.ds(pl.multiple_of(g * HS, HS), HS)
-            other = ch * 2 + (1 - c)
-            same = ch * 2 + c
-            remote(
-                oh.at[rows(other, TD), :], lat_out.at[:, mine], sem_send.at[3], sem_recv.at[3], other
-            ).start()
-
-            @pl.when(ch != chip)
-            def _():
-                remote(
-                    oh.at[rows(same, TD), :], lat_out.at[:, mine], sem_send.at[3], sem_recv.at[3], same
-                ).start()
-
-            @pl.when(ch == chip)
-            def _():
-                pltpu.make_async_copy(
-                    oh.at[rows(same, TD), :], lat_out.at[:, mine], sem_recv.at[3]
-                ).start()
-
         if i_s is not None:
             return jnp.max(top, axis=1, keepdims=True)
 
     drain(kh, sem_recv.at[0])
     peak0 = step(0, sa, None, None, None)
-    drain(vh, sem_recv.at[1])
 
     @pl.loop(0, 7, init_carry=peak0)
     def fwd(i, peak):
@@ -198,7 +176,63 @@
     peak15 = step(15, sb, 14, sa, fwd)
     step(None, None, 15, sb, peak15)
 
-    pooled = mm(member[...], oh[...], NN) * inv_count
+    bt = 512
+    inv_scale = 1.0 / math.sqrt(HS)
+    mine = pl.ds(pl.multiple_of(g * HS, HS), HS)
+
+    def pair(i):
+        return rows(q_chip(2 * i, -1), bq), rows(q_chip(2 * i + 1, -1), bq)
+
+    def load_rows(ref, i, cols=slice(None)):
+        r0, r1 = pair(i)
+        return jnp.concatenate([ref[r0, cols], ref[r1, cols]], axis=0)
+
+    def load_cols(ref, i):
+        r0, r1 = pair(i)
+        return jnp.concatenate([ref[:, r0], ref[:, r1]], axis=1)
+
+    def store_rows(ref, i, value):
+        r0, r1 = pair(i)
+        ref[r0, :] = value[:bq]
+        ref[r1, :] = value[bq:]
+
+    def row_factor(i, factor):
+        return jnp.transpose(jnp.broadcast_to(load_cols(wrow, i) * factor, (HS, bt)))
+
+    def give(src, ch, out, which):
+        other = ch * 2 + (1 - c)
+        same = ch * 2 + c
+        remote(
+            src.at[rows(other, TD), :], out.at[:, mine], sem_send.at[which], sem_recv.at[which], other
+        ).start()
+
+        @pl.when(ch != chip)
+        def _():
+            remote(
+                src.at[rows(same, TD), :], out.at[:, mine], sem_send.at[which], sem_recv.at[which], same
+            ).start()
+
+        @pl.when(ch == chip)
+        def _():
+            pltpu.make_async_copy(
+                src.at[rows(same, TD), :], out.at[:, mine], sem_recv.at[which]
+            ).start()
+
+    def give_pair(src, i, out, which):
+        give(src, q_chip(2 * i, -1), out, which)
+        give(src, q_chip(2 * i + 1, -1), out, which)
+
+    memberl[...] = (member[...].astype(f32) * wrow[...]).astype(bf16)
+    drain(vh, sem_recv.at[1])
+
+    @pl.loop(0, TOK // bt, init_carry=jnp.zeros((FP, HS), f32))
+    def pooled_sum(i, total):
+        o = (mm(load_rows(probs, i), vh[...], NN) * row_factor(i, 1.0)).astype(bf16)
+        store_rows(oh, i, o)
+        give_pair(oh, i, lat_out, 3)
+        return total + mm(load_cols(member, i), o, NN)
+
+    pooled = pooled_sum * inv_count
     square = jnp.sum(pooled * pooled, axis=1, keepdims=True)
     pooled_b = pooled.astype(bf16)
     for n in range(DH // 512):
@@ -235,7 +269,6 @@
             cols = pl.ds(n * 512, 512)
             rbuf[:, cols] = mm(memberl[...], probs[:, cols], NN).astype(bf16)
 
-    memberl[...] = (member[...].astype(f32) * wrow[...]).astype(bf16)
     frame_sums(0, 4)
 
     @pl.when(owner < OWN)
@@ -292,101 +325,35 @@
         p = peer(off)
         remote(g_src, g_all.at[rows(g, FP), :], sem_send.at[7], sem_recv.at[7], p).start()
 
-    bt = 512
-    half = TOK // bt // 2
+    first = 8
     cb = 1024
-    inv_scale = 1.0 / math.sqrt(HS)
-    mine = pl.ds(pl.multiple_of(g * HS, HS), HS)
-    spin = g // 4
-
-    def give(src, p, out, which):
-        @pl.when(p != g)
-        def _():
-            remote(
-                src.at[rows(p, TD), :], out.at[:, mine], sem_send.at[which], sem_recv.at[which], p
-            ).start()
-
-        @pl.when(p == g)
-        def _():
-            pltpu.make_async_copy(
-                src.at[rows(p, TD), :], out.at[:, mine], sem_recv.at[which]
-            ).start()
-
-    def block_of(i):
-        return (i + spin) % (TOK // bt)
-
-    def grads_of(r):
-        grad_rows = mm(member[:, r], g_src[...], TN)
-        delta = jnp.sum(grad_rows * oh[r, :].astype(f32), axis=1, keepdims=True)
-        return grad_rows.astype(bf16), delta
-
-    def scaled_q(r):
-        return (qwt[:, r].astype(f32) * (wrow[:, r] * inv_scale)).astype(bf16)
-
-    def finish_q(r, acc):
-        w_cols = jnp.transpose(jnp.broadcast_to(wrow[:, r] * inv_scale, (HS, bt)))
-        qh[r, :] = (acc * w_cols).astype(bf16)
-
-    def part(j, k):
-        return pl.ds((2 * j + k) * HS, HS)
-
-    def store_part(ref, j, value):
-        ref[:, part(j, 0)] = value[:bq, :]
-        ref[:, part(j, 1)] = value[bq:, :]
-
-    def load_part(ref, j):
-        return jnp.concatenate([ref[:, part(j, 0)], ref[:, part(j, 1)]], axis=0)
-
     dkt[...] = jnp.zeros_like(dkt)
 
-    @pl.loop(0, half)
+    def grads_of(i):
+        grad_rows = mm(load_cols(member, i), g_src[...], TN)
+        delta = jnp.sum(grad_rows * load_rows(oh, i).astype(f32), axis=1, keepdims=True)
+        qb = (load_cols(qwt, i).astype(f32) * (load_cols(wrow, i) * inv_scale)).astype(bf16)
+        return grad_rows.astype(bf16), delta, qb
+
+    @pl.loop(0, first)
     def _(i):
-        blk = block_of(i)
-        r = rows(blk, bt)
-        grad_b, delta = grads_of(r)
+        grad_b, delta, qb = grads_of(i)
         acc = jnp.zeros((bt, HS), f32)
-        qb = scaled_q(r)
         for n in range(TOK // cb):
             cols = pl.ds(n * cb, cb)
             dp = mm(grad_b, vh[cols, :], NT)
-            ds = (dp - delta).astype(bf16) * probs[r, cols]
+            ds = (dp - delta).astype(bf16) * load_rows(probs, i, cols)
             acc = acc + mm(ds, kh[cols, :], NN)
             dkt[:, cols] += mm(qb, ds, NN)
-        finish_q(r, acc)
-        for d in range(bt // TD):
-            give(qh, blk * (bt // TD) + d, dq_out, 9)
-
-    for j in range(half):
-        r = rows(block_of(half + j), bt)
-        grad_b, delta = grads_of(r)
-        dob[j * bt:(j + 1) * bt, :] = grad_b
-        store_part(sb, j, jnp.broadcast_to(delta, (bt, HS)))
-        store_part(sa, j, jnp.zeros((bt, HS), f32))
-        qwt[:, r] = scaled_q(r)
-
-    @pl.loop(0, TOK // bt)
+        store_rows(qh, i, (acc * row_factor(i, inv_scale)).astype(bf16))
+        give_pair(qh, i, dq_out, 9)
+
+    @pl.loop(0, 16)
     def _(i):
-        blk = block_of(i)
-        cols = rows(blk, bt)
-        kc = kh[cols, :]
-        vc = vh[cols, :]
-        dk = dkt[:, cols]
-        for j in range(half):
-            r = rows(block_of(half + j), bt)
-            jr = slice(j * bt, (j + 1) * bt)
-            dp = mm(dob[jr, :], vc, NT)
-            ds = (dp - load_part(sb, j)[:, 0:1]).astype(bf16) * probs[r, cols]
-            store_part(sa, j, load_part(sa, j) + mm(ds, kc, NN))
-            dk = dk + mm(qwt[:, r], ds, NN)
-        kh[cols, :] = jnp.transpose(dk).astype(bf16)
-        for d in range(bt // TD):
-            give(kh, blk * (bt // TD) + d, dk_out, 10)
-
-    for j in range(half):
-        blk = block_of(half + j)
-        finish_q(rows(blk, bt), load_part(sa, j))
-        for d in range(bt // TD):
-            give(qh, blk * (bt // TD) + d, dq_out, 9)
+        ch = q_chip(i, -1)
+        r = rows(ch, bq)
+        kh[r, :] = jnp.transpose(dkt[:, r]).astype(bf16)
+        give(kh, ch, dk_out, 10)
 
     for n in range(DH // 512):
         cols = pl.ds(n * 512, 512)
@@ -438,19 +405,28 @@
 
 
 def settle(*refs):
-    sem = refs[-1]
-    n = (len(refs) - 1) // 2
-    copies = []
+    n = 5
+    ins, outs, bufs = refs[:n], refs[n:2 * n], refs[2 * n:3 * n]
+    sem_in, sem_out = refs[3 * n:]
+    pieces = []
     for i in range(n):
         parts = 4 if i < n - 1 else 1
-        step = refs[i].shape[0] // parts
-        for j in range(parts):
-            r = pl.ds(j * step, step)
-            copy = pltpu.make_async_copy(refs[i].at[r], refs[n + i].at[r], sem.at[len(copies)])
-            copy.start()
-            copies.append(copy)
-    for copy in copies:
-        copy.wait()
+        step = ins[i].shape[0] // parts
+        pieces += [(i, pl.ds(j * step, step)) for j in range(parts)]
+    moves = [
+        (
+            pltpu.make_async_copy(ins[i].at[r], bufs[i].at[r], sem_in.at[m]),
+            pltpu.make_async_copy(bufs[i].at[r], outs[i].at[r], sem_out.at[m]),
+        )
+        for m, (i, r) in enumerate(pieces)
+    ]
+    for fetch, _ in moves:
+        fetch.start()
+    for fetch, put in moves:
+        fetch.wait()
+        put.start()
+    for _, put in moves:
+        put.wait()
 
 
 def on_device(
@@ -479,7 +455,6 @@
             V((FP, DH + OT), bf16), V((GEN * FP, OT), bf16), V((FP, OT), bf16),
             V((FP, DH + OT), bf16), V((FP, DH), f32), V((FP, DH), f32),
             V((16, DH), bf16), V((GRP * 16, DH), bf16),
-            V((TOK // 2, HS), bf16),
             pltpu.SemaphoreType.DMA((11,)),
             pltpu.SemaphoreType.DMA((16,)),
             pltpu.SemaphoreType.DMA((11,)),
@@ -497,7 +472,7 @@
         out_shape=tuple(jax.ShapeDtypeStruct(o.shape, o.dtype) for o in outs),
         in_specs=[hbm] * 5,
         out_specs=(hbm,) * 5,
-        scratch_shapes=[pltpu.SemaphoreType.DMA((17,))],
+        scratch_shapes=[V(o.shape, o.dtype) for o in outs] + [pltpu.SemaphoreType.DMA((17,))] * 2,
         name="settle",
     )(*outs)
     return (lat[None], dq[None], dk[None], dv[None], gh)

time: 268 us -> 132 us (0.49)
  Pallas kernels: 266 us -> 131 us
    pallas_call x1, Pallas kernels: 133 us -> 4 us  [on_device(): pl.pallas_call(settle, out_shape=tuple((jax.ShapeDtypeStruct(o.shape, o.d...]
    pallas_call x1, Pallas kernels: 133 us -> 127 us  [on_device(): pl.pallas_call(body, out_shape=(rows_shape, rows_shape, rows_shape, rows_...]
where the time goes in v3:
time: 132 us
  Pallas kernels  131 us (99%)
  between operations  1.45 us (1%)
    pallas_call x1, Pallas kernels, on_device(): pl.pallas_call(body, out_shape=(rows_shape, rows_shape, rows_shape, rows_...  127 us
    pallas_call x1, Pallas kernels, on_device(): pl.pallas_call(settle, out_shape=tuple((jax.ShapeDtypeStruct(o.shape, o.d...  4 us

profile of v3, /device:TPU:1, one launch (start us, length us, event | category | flops | bytes accessed | tf_op | source)
XLA Modules:
  0.0 132.1 jit_solution(12671643430908179515)
XLA Ops:
  1.3 126.7 %clip_step.1 = (bf16[128,4096]{1,0:T(8,128)(2,1)}, bf16[128,4096]{1,0:T(8,128)(2,1)}, bf16[128,4096]{1,0:T(8,128)(2,1)}, bf16[128,4096]{1,0:T(8,128)(2,1)}, f32[8,5120]{1,0:T(8,128)}) custom-call(bf16[128,4096]{1,0:T(8,128)(2,1)} %bitcast.7, bf16[128,4096]{1,0:T(8,128)(2,1)} %bitcast.8, bf16[128,4096]{1,0:T(8,128)(2,1)} %bitcast.9, bf16[128,5120]{1,0:T(8,128)(2,1)} %w_ref.1, ...), custom_call_target="tpu_custom_call" | custom-call | tf_op jit(solution)/shard_map/clip_step/pallas_call | solution.py:440
  127.9 4.0 %settle.1 = (bf16[128,4096]{1,0:T(8,128)(2,1)}, bf16[128,4096]{1,0:T(8,128)(2,1)}, bf16[128,4096]{1,0:T(8,128)(2,1)}, bf16[128,4096]{1,0:T(8,128)(2,1)}, f32[8,5120]{1,0:T(8,128)}) custom-call(bf16[128,4096]{1,0:T(8,128)(2,1)} %get-tuple-element.15.refs_0_, bf16[128,4096]{1,0:T(8,128)(2,1)} %get-tuple-element.16.refs_1_, ...), custom_call_target="tpu_custom_call" | custom-call | tf_op jit(solution)/shard_map/settle/pallas_call | solution.py:470

commit v4 on v3

--- a/solution.py
+++ b/solution.py
@@ -42,7 +42,7 @@
     q_in, k_in, v_in, w_ref, disc_ref, frames_ref, hof_ref, time_ref,
     lat_out, dq_out, dk_out, dv_out, gh_out,
     probs, qh, kh, vh, oh, sa, sb, dkt, qwt, wrow, member, memberl, rbuf, r_all, g_src, g_all,
-    rs_src, rs_recv, ag_src, proj, head_rows, gsf, hp_src, hp_all,
+    rs_src, rs_recv, ag_src, proj, head_rows, gsf, hp_src, hp_all, dob,
     sem_send, sem_q, sem_recv,
 ):
     g = lax.axis_index("gen")
@@ -229,7 +229,11 @@
     def pooled_sum(i, total):
         o = (mm(load_rows(probs, i), vh[...], NN) * row_factor(i, 1.0)).astype(bf16)
         store_rows(oh, i, o)
-        give_pair(oh, i, lat_out, 3)
+
+        @pl.when(i < 5)
+        def _():
+            give_pair(oh, i, lat_out, 3)
+
         return total + mm(load_cols(member, i), o, NN)
 
     pooled = pooled_sum * inv_count
@@ -245,11 +249,17 @@
         return jnp.where(lane_o == 0, high, jnp.where(lane_o == 1, value - high, 0.0))
 
     rs_src[:, DH:] = high_low(square).astype(bf16)
-    owner = chip + 16 * c
+
+    def owner_of(p):
+        ch = p // 2
+        second = jnp.where(ch % 5 == 0, 16 + ch // 5, jnp.where(ch == 4, OWN - 1, 2 * OWN))
+        return jnp.where(p % 2 == 0, ch, second)
+
+    owner = owner_of(g)
 
     for off in FAR:
         p = peer(off)
-        o = p // 2 + 16 * (p % 2)
+        o = owner_of(p)
 
         @pl.when(o < OWN)
         def _():
@@ -288,12 +298,6 @@
             ).start()
 
     frame_sums(4, 8)
-    pltpu.make_async_copy(rbuf.at[:, rows(g, TD)], r_all.at[rows(g, FP), :], sem_recv.at[6]).start()
-    for off in FAR:
-        p = peer(off)
-        remote(
-            rbuf.at[:, rows(p, TD)], r_all.at[rows(g, FP), :], sem_send.at[6], sem_recv.at[6], p
-        ).start()
     drain(proj, sem_recv.at[5])
 
     squares = proj[:, DH:DH + 128].astype(f32)
@@ -325,7 +329,16 @@
         p = peer(off)
         remote(g_src, g_all.at[rows(g, FP), :], sem_send.at[7], sem_recv.at[7], p).start()
 
-    first = 8
+    for i in range(5, 8):
+        give_pair(oh, i, lat_out, 3)
+    pltpu.make_async_copy(rbuf.at[:, rows(g, TD)], r_all.at[rows(g, FP), :], sem_recv.at[6]).start()
+    for off in FAR:
+        p = peer(off)
+        remote(
+            rbuf.at[:, rows(p, TD)], r_all.at[rows(g, FP), :], sem_send.at[6], sem_recv.at[6], p
+        ).start()
+
+    first = 4
     cb = 1024
     dkt[...] = jnp.zeros_like(dkt)
 
@@ -348,12 +361,48 @@
         store_rows(qh, i, (acc * row_factor(i, inv_scale)).astype(bf16))
         give_pair(qh, i, dq_out, 9)
 
-    @pl.loop(0, 16)
+    def part(j, k):
+        return pl.ds((2 * j + k) * HS, HS)
+
+    def store_part(ref, j, value):
+        ref[:, part(j, 0)] = value[:bq, :]
+        ref[:, part(j, 1)] = value[bq:, :]
+
+    def load_part(ref, j):
+        return jnp.concatenate([ref[:, part(j, 0)], ref[:, part(j, 1)]], axis=0)
+
+    rest = TOK // bt - first
+    for j in range(rest):
+        grad_b, delta, qb = grads_of(first + j)
+        dob[j * bt:(j + 1) * bt, :] = grad_b
+        store_part(sb, j, jnp.broadcast_to(delta, (bt, HS)))
+        store_part(sa, j, jnp.zeros((bt, HS), f32))
+        r0, r1 = pair(first + j)
+        qwt[:, r0] = qb[:, :bq]
+        qwt[:, r1] = qb[:, bq:]
+
+    @pl.loop(0, 4)
     def _(i):
-        ch = q_chip(i, -1)
-        r = rows(ch, bq)
-        kh[r, :] = jnp.transpose(dkt[:, r]).astype(bf16)
-        give(kh, ch, dk_out, 10)
+        chips = [q_chip(4 * i + m, -1) for m in range(4)]
+        spans = [rows(ch, bq) for ch in chips]
+        kc = jnp.concatenate([kh[r, :] for r in spans], axis=0)
+        vc = jnp.concatenate([vh[r, :] for r in spans], axis=0)
+        for j in range(rest):
+            dp = mm(dob[j * bt:(j + 1) * bt, :], vc, NT)
+            pb = jnp.concatenate([load_rows(probs, first + j, r) for r in spans], axis=1)
+            ds = (dp - load_part(sb, j)[:, 0:1]).astype(bf16) * pb
+            store_part(sa, j, load_part(sa, j) + mm(ds, kc, NN))
+            dk = mm(load_cols(qwt, first + j), ds, NN)
+            for m in range(4):
+                dkt[:, spans[m]] += dk[:, m * bq:(m + 1) * bq]
+        for m in range(4):
+            kh[spans[m], :] = jnp.transpose(dkt[:, spans[m]]).astype(bf16)
+            give(kh, chips[m], dk_out, 10)
+
+    for j in range(rest):
+        i = first + j
+        store_rows(qh, i, (load_part(sa, j) * row_factor(i, inv_scale)).astype(bf16))
+        give_pair(qh, i, dq_out, 9)
 
     for n in range(DH // 512):
         cols = pl.ds(n * 512, 512)
@@ -455,6 +504,7 @@
             V((FP, DH + OT), bf16), V((GEN * FP, OT), bf16), V((FP, OT), bf16),
             V((FP, DH + OT), bf16), V((FP, DH), f32), V((FP, DH), f32),
             V((16, DH), bf16), V((GRP * 16, DH), bf16),
+            V((TOK // 2, HS), bf16),
             pltpu.SemaphoreType.DMA((11,)),
             pltpu.SemaphoreType.DMA((16,)),
             pltpu.SemaphoreType.DMA((11,)),

time: 132 us -> 126 us (0.955)
  Pallas kernels: 131 us -> 124 us
    pallas_call x1, Pallas kernels: 127 us -> 120 us  [on_device(): pl.pallas_call(body, out_shape=(rows_shape, rows_shape, rows_shape, rows_...]
where the time goes in v4:
time: 126 us
  Pallas kernels  124 us (98%)
  between operations  1.45 us (1%)
    pallas_call x1, Pallas kernels, on_device(): pl.pallas_call(body, out_shape=(rows_shape, rows_shape, rows_shape, rows_...  120 us
    pallas_call x1, Pallas kernels, on_device(): pl.pallas_call(settle, out_shape=tuple((jax.ShapeDtypeStruct(o.shape, o.d...  4 us

profile of v4, /device:TPU:1, one launch (start us, length us, event | category | flops | bytes accessed | tf_op | source)
XLA Modules:
  0.0 125.8 jit_solution(15385321036076687524)
XLA Ops:
  1.3 120.4 %clip_step.1 = (bf16[128,4096]{1,0:T(8,128)(2,1)}, bf16[128,4096]{1,0:T(8,128)(2,1)}, bf16[128,4096]{1,0:T(8,128)(2,1)}, bf16[128,4096]{1,0:T(8,128)(2,1)}, f32[8,5120]{1,0:T(8,128)}) custom-call(bf16[128,4096]{1,0:T(8,128)(2,1)} %bitcast.7, bf16[128,4096]{1,0:T(8,128)(2,1)} %bitcast.8, bf16[128,4096]{1,0:T(8,128)(2,1)} %bitcast.9, bf16[128,5120]{1,0:T(8,128)(2,1)} %w_ref.1, ...), custom_call_target="tpu_custom_call" | custom-call | tf_op jit(solution)/shard_map/clip_step/pallas_call | solution.py:489
  121.7 4.0 %settle.1 = (bf16[128,4096]{1,0:T(8,128)(2,1)}, bf16[128,4096]{1,0:T(8,128)(2,1)}, bf16[128,4096]{1,0:T(8,128)(2,1)}, bf16[128,4096]{1,0:T(8,128)(2,1)}, f32[8,5120]{1,0:T(8,128)}) custom-call(bf16[128,4096]{1,0:T(8,128)(2,1)} %get-tuple-element.15.refs_0_, bf16[128,4096]{1,0:T(8,128)(2,1)} %get-tuple-element.16.refs_1_, ...), custom_call_target="tpu_custom_call" | custom-call | tf_op jit(solution)/shard_map/settle/pallas_call | solution.py:520

commit v5 on v4

--- a/solution.py
+++ b/solution.py
@@ -96,16 +96,6 @@
             ).start()
 
     gather_rows(k_in, kh, 0)
-    pltpu.make_async_copy(q_in.at[:, rows(g, TD)], qh.at[rows(g, TD), :], sem_q.at[0]).start()
-    for i in range(16):
-        for dc in (0, 1):
-            if i == 0 and dc == 0:
-                continue
-            p = q_chip(i, 1) * 2 + (c + dc) % 2
-            remote(
-                q_in.at[:, rows(p, TD)], qh.at[rows(g, TD), :], sem_send.at[2], sem_q.at[i], p
-            ).start()
-    gather_rows(v_in, vh, 1)
 
     frames = frames_ref[...]
     mem = (frames == lax.broadcasted_iota(jnp.int32, (FP, TOK), 0)).astype(f32)
@@ -134,6 +124,16 @@
             part = part - high.astype(f32)
         head_rows[:, cols] = total
 
+    pltpu.make_async_copy(q_in.at[:, rows(g, TD)], qh.at[rows(g, TD), :], sem_q.at[0]).start()
+    for i in range(16):
+        for dc in (0, 1):
+            if i == 0 and dc == 0:
+                continue
+            p = q_chip(i, 1) * 2 + (c + dc) % 2
+            remote(
+                q_in.at[:, rows(p, TD)], qh.at[rows(g, TD), :], sem_send.at[2], sem_q.at[i], p
+            ).start()
+
     scale2 = math.log2(math.e) / math.sqrt(HS)
     ck = 512
     bq = 256
@@ -166,6 +166,7 @@
             return jnp.max(top, axis=1, keepdims=True)
 
     drain(kh, sem_recv.at[0])
+    gather_rows(v_in, vh, 1)
     peak0 = step(0, sa, None, None, None)
 
     @pl.loop(0, 7, init_carry=peak0)

time: 126 us -> 123 us (0.976)
  Pallas kernels: 124 us -> 121 us
    pallas_call x1, Pallas kernels: 120 us -> 117 us  [on_device(): pl.pallas_call(body, out_shape=(rows_shape, rows_shape, rows_shape, rows_...]
where the time goes in v5:
time: 123 us
  Pallas kernels  121 us (98%)
  between operations  1.45 us (1%)
    pallas_call x1, Pallas kernels, on_device(): pl.pallas_call(body, out_shape=(rows_shape, rows_shape, rows_shape, rows_...  117 us
    pallas_call x1, Pallas kernels, on_device(): pl.pallas_call(settle, out_shape=tuple((jax.ShapeDtypeStruct(o.shape, o.d...  4 us

profile of v5, /device:TPU:1, one launch (start us, length us, event | category | flops | bytes accessed | tf_op | source)
XLA Modules:
  0.0 122.5 jit_solution(16934035271707747507)
XLA Ops:
  1.3 117.1 %clip_step.1 = (bf16[128,4096]{1,0:T(8,128)(2,1)}, bf16[128,4096]{1,0:T(8,128)(2,1)}, bf16[128,4096]{1,0:T(8,128)(2,1)}, bf16[128,4096]{1,0:T(8,128)(2,1)}, f32[8,5120]{1,0:T(8,128)}) custom-call(bf16[128,4096]{1,0:T(8,128)(2,1)} %bitcast.7, bf16[128,4096]{1,0:T(8,128)(2,1)} %bitcast.8, bf16[128,4096]{1,0:T(8,128)(2,1)} %bitcast.9, bf16[128,5120]{1,0:T(8,128)(2,1)} %w_ref.1, ...), custom_call_target="tpu_custom_call" | custom-call | tf_op jit(solution)/shard_map/clip_step/pallas_call | solution.py:490
  118.4 4.0 %settle.1 = (bf16[128,4096]{1,0:T(8,128)(2,1)}, bf16[128,4096]{1,0:T(8,128)(2,1)}, bf16[128,4096]{1,0:T(8,128)(2,1)}, bf16[128,4096]{1,0:T(8,128)(2,1)}, f32[8,5120]{1,0:T(8,128)}) custom-call(bf16[128,4096]{1,0:T(8,128)(2,1)} %get-tuple-element.15.refs_0_, bf16[128,4096]{1,0:T(8,128)(2,1)} %get-tuple-element.16.refs_1_, ...), custom_call_target="tpu_custom_call" | custom-call | tf_op jit(solution)/shard_map/settle/pallas_call | solution.py:521

commit v6 on v5

--- a/solution.py
+++ b/solution.py
@@ -226,16 +226,22 @@
     memberl[...] = (member[...].astype(f32) * wrow[...]).astype(bf16)
     drain(vh, sem_recv.at[1])
 
-    @pl.loop(0, TOK // bt, init_carry=jnp.zeros((FP, HS), f32))
+    @pl.loop(0, TOK // (2 * bt), init_carry=jnp.zeros((FP, HS), f32))
     def pooled_sum(i, total):
-        o = (mm(load_rows(probs, i), vh[...], NN) * row_factor(i, 1.0)).astype(bf16)
-        store_rows(oh, i, o)
-
-        @pl.when(i < 5)
+        pairs = (2 * i, 2 * i + 1)
+        weights = jnp.concatenate([load_rows(probs, j) for j in pairs], axis=0)
+        product = mm(weights, vh[...], NN)
+        for n, j in enumerate(pairs):
+            o = (product[n * bt:(n + 1) * bt, :] * row_factor(j, 1.0)).astype(bf16)
+            store_rows(oh, j, o)
+            total = total + mm(load_cols(member, j), o, NN)
+
+        @pl.when(i < 2)
         def _():
-            give_pair(oh, i, lat_out, 3)
-
-        return total + mm(load_cols(member, i), o, NN)
+            for j in pairs:
+                give_pair(oh, j, lat_out, 3)
+
+        return total
 
     pooled = pooled_sum * inv_count
     square = jnp.sum(pooled * pooled, axis=1, keepdims=True)
@@ -330,7 +336,7 @@
         p = peer(off)
         remote(g_src, g_all.at[rows(g, FP), :], sem_send.at[7], sem_recv.at[7], p).start()
 
-    for i in range(5, 8):
+    for i in range(4, 8):
         give_pair(oh, i, lat_out, 3)
     pltpu.make_async_copy(rbuf.at[:, rows(g, TD)], r_all.at[rows(g, FP), :], sem_recv.at[6]).start()
     for off in FAR:
@@ -460,7 +466,7 @@
     sem_in, sem_out = refs[3 * n:]
     pieces = []
     for i in range(n):
-        parts = 4 if i < n - 1 else 1
+        parts = 2 if i < n - 1 else 1
         step = ins[i].shape[0] // parts
         pieces += [(i, pl.ds(j * step, step)) for j in range(parts)]
     moves = [
@@ -523,7 +529,7 @@
         out_shape=tuple(jax.ShapeDtypeStruct(o.shape, o.dtype) for o in outs),
         in_specs=[hbm] * 5,
         out_specs=(hbm,) * 5,
-        scratch_shapes=[V(o.shape, o.dtype) for o in outs] + [pltpu.SemaphoreType.DMA((17,))] * 2,
+        scratch_shapes=[V(o.shape, o.dtype) for o in outs] + [pltpu.SemaphoreType.DMA((9,))] * 2,
         name="settle",
     )(*outs)
     return (lat[None], dq[None], dk[None], dv[None], gh)

time: 123 us -> 120 us (0.976)
  Pallas kernels: 121 us -> 119 us
    pallas_call x1, Pallas kernels: 117 us -> 115 us  [on_device(): pl.pallas_call(body, out_shape=(rows_shape, rows_shape, rows_shape, rows_...]
where the time goes in v6:
time: 120 us
  Pallas kernels  119 us (99%)
  between operations  1.45 us (1%)
    pallas_call x1, Pallas kernels, on_device(): pl.pallas_call(body, out_shape=(rows_shape, rows_shape, rows_shape, rows_...  115 us
    pallas_call x1, Pallas kernels, on_device(): pl.pallas_call(settle, out_shape=tuple((jax.ShapeDtypeStruct(o.shape, o.d...  3.64 us

profile of v6, /device:TPU:1, one launch (start us, length us, event | category | flops | bytes accessed | tf_op | source)
XLA Modules:
  0.0 120.1 jit_solution(16162617791606280664)
XLA Ops:
  1.3 115.0 %clip_step.1 = (bf16[128,4096]{1,0:T(8,128)(2,1)}, bf16[128,4096]{1,0:T(8,128)(2,1)}, bf16[128,4096]{1,0:T(8,128)(2,1)}, bf16[128,4096]{1,0:T(8,128)(2,1)}, f32[8,5120]{1,0:T(8,128)}) custom-call(bf16[128,4096]{1,0:T(8,128)(2,1)} %bitcast.7, bf16[128,4096]{1,0:T(8,128)(2,1)} %bitcast.8, bf16[128,4096]{1,0:T(8,128)(2,1)} %bitcast.9, bf16[128,5120]{1,0:T(8,128)(2,1)} %w_ref.1, ...), custom_call_target="tpu_custom_call" | custom-call | tf_op jit(solution)/shard_map/clip_step/pallas_call | solution.py:496
  116.3 3.6 %settle.1 = (bf16[128,4096]{1,0:T(8,128)(2,1)}, bf16[128,4096]{1,0:T(8,128)(2,1)}, bf16[128,4096]{1,0:T(8,128)(2,1)}, bf16[128,4096]{1,0:T(8,128)(2,1)}, f32[8,5120]{1,0:T(8,128)}) custom-call(bf16[128,4096]{1,0:T(8,128)(2,1)} %get-tuple-element.15.refs_0_, bf16[128,4096]{1,0:T(8,128)(2,1)} %get-tuple-element.16.refs_1_, ...), custom_call_target="tpu_custom_call" | custom-call | tf_op jit(solution)/shard_map/settle/pallas_call | solution.py:527
